TPU v7x, 256 devices: a whole 4x4x8 slice. The times are simulated.
256 devices in a mesh: row: 32 (over z, y_lo, core), col: 8 (over x, y_hi).
Axes of the slice: x: 4, y: 4 (y_hi: 2, y_lo: 2; y = y_hi * 2 + y_lo), z: 8, core: 2. Of those that a mesh axis runs over, the one named last changes fastest.
Arguments:
- acts: bfloat16 [1024, 16384], P(None, 'col'), may hold values from -6 to 6
- grads: bfloat16 [1024, 16384], P(None, 'row'), may hold values from -0.1875 to 0.1875
- row_roots: bfloat16 [16384, 1024], P('row'), as said below
- col_stats: float32 [1024, 16384], P('row', 'col'), as said below
Outputs:
- update: bfloat16 [16384, 16384], P('row', 'col')
- new_stats: float32 [1024, 16384], P('row', 'col')
- new_roots: float32 [1024, 16384], P('row', 'col')
Inputs may be any that keep to these rules, and one draw needn't show every extreme that they name: `col_stats`: each block of 1024 columns is symmetric positive definite. `row_roots`: each block of 1024 rows is symmetric.
All inputs are finite; a program needn't handle non-finite values.
Results may differ from a plain program's by a relative error of at most 0.0015.
The roundings to bfloat16 on the way count: a program that leaves them out, or rounds other values in their place, can miss the bound.
Values may be sent and summed in bfloat16 or wider, within the bound.
No kernel may reach another device: no remote copies, remote signals or barrier semaphores. Data moves between devices by JAX's collectives and lax.ppermute only.
A program may use at most 128 MiB of HBM per device.

v0:
```python
import jax
import jax.numpy as jnp
from jax import lax
from jax.sharding import Mesh, PartitionSpec as P
from jax.experimental import pallas as pl
from jax.experimental.pallas import tpu as pltpu

decay_rate = 0.75
damping = 0.001
epsilon = 1e-06
TILE = 256
SLAB = 128
DISTANCES = 5
f32 = jnp.float32
bf16 = jnp.bfloat16


def tdot(a, b):
    return lax.dot_general(a, b, (((0,), (0,)), ((), ())), preferred_element_type=f32)


def dot(a, b):
    return jnp.dot(a, b, preferred_element_type=f32)


def tiles(count, body):
    def turn(j, carry):
        body(pl.ds(pl.multiple_of(j * TILE, TILE), TILE), j)
        return carry

    lax.fori_loop(0, count, turn, 0)


def for_halves(body, half):
    def turn(i, carry):
        body(pl.ds(pl.multiple_of(i * half, half), half), i)
        return carry

    lax.fori_loop(0, 2, turn, 0)


def held(shape, index=None):
    index = index or (lambda i, s: (0,) * len(shape))
    return pl.BlockSpec(shape, index, pipeline_mode=pl.Buffered(1))


def scalar():
    return pl.BlockSpec(memory_space=pltpu.SMEM)


def call(kernel, outs, out_specs, in_specs, scratch, limit, flops, name):
    return pl.pallas_call(
        kernel,
        out_shape=[jax.ShapeDtypeStruct(*o) for o in outs],
        grid_spec=pltpu.PrefetchScalarGridSpec(
            num_scalar_prefetch=1,
            grid=(1,),
            in_specs=in_specs,
            out_specs=out_specs,
            scratch_shapes=scratch,
        ),
        compiler_params=pltpu.CompilerParams(vmem_limit_bytes=limit << 20),
        cost_estimate=pl.CostEstimate(flops=flops, bytes_accessed=8 << 20, transcendentals=0),
        name=name,
    )


def slab(ids, k):
    return lax.rem(ids[1] + k, 8)


def fill_grad(g, acts, grad, first, gsq):
    half = g.shape[1]

    def fill(cols, j):
        t = tdot(g[...], acts[:, cols]).astype(bf16)
        grad[pl.ds(first, half), cols] = t
        gsq[0, 0] += jnp.sum(jnp.square(t.astype(f32)))

    tiles(acts.shape[1] // TILE, fill)


def whiten_kernel(ids, acts, g_own, g_other, r_own, r_other, wide, gsq, *rest):
    pieces, grad = rest[:-1], rest[-1]
    core = ids[0]
    half = g_own.shape[1]
    size = acts.shape[1]
    cut = SLAB // 2
    gsq[0, 0] = 0.0
    for g, who in ((g_own, core), (g_other, 1 - core)):
        fill_grad(g, acts, grad, pl.multiple_of(who * half, half), gsq)
    for r, who in ((r_own, core), (r_other, 1 - core)):
        first = pl.multiple_of(who * half, half)

        def fill_white(cols, j):
            wide[pl.ds(first, half), cols] = dot(r[...], grad[:, cols]).astype(bf16)

        tiles(size // TILE, fill_white)
    wide[:, size:] = wide[:, : (DISTANCES - 1) * SLAB]
    for k in range(size // SLAB):
        first = pl.multiple_of(slab(ids, k) * SLAB, SLAB)
        t = tdot(wide[:, pl.ds(first, SLAB)], wide[:, pl.ds(first, DISTANCES * SLAB)])
        pieces[2 * k][...] = t[:cut]
        pieces[2 * k + 1][...] = t[cut:]


WHITEN_MIB = 48
PIECE = (SLAB // 2, DISTANCES * SLAB)


def whiten(ids, acts, g_own, g_other, r_own, r_other):
    tok, half = g_own.shape
    size = acts.shape[1]
    count = 2 * size // SLAB
    wide = (size, size + (DISTANCES - 1) * SLAB)
    return call(
        whiten_kernel,
        [(wide, bf16), ((1, 1), f32)] + [(PIECE, f32)] * count,
        [held(wide), scalar()] + [held(PIECE)] * count,
        [held((tok, size))] + [held((tok, half))] * 2 + [held((half, size))] * 2,
        [pltpu.VMEM((size, size), bf16)],
        WHITEN_MIB,
        2 * size * size * (tok + size + DISTANCES * SLAB),
        "whiten",
    )(ids, acts, g_own, g_other, r_own, r_other)


def halves(x):
    high = x.astype(bf16)
    return high, (x - high.astype(f32)).astype(bf16)


def eye_tile(shape, row, col):
    return (
        lax.broadcasted_iota(jnp.int32, shape, 0) + row
        == lax.broadcasted_iota(jnp.int32, shape, 1) + col
    )


def root_kernel(ids, gsq, *refs):
    slabs = 8
    pieces = refs[: 2 * slabs]
    part_a, part_b, rh, kept_rows, squares = refs[2 * slabs : 2 * slabs + 5]
    y, yh, yl, zh, zl, qh, ql, root = refs[2 * slabs + 5 :]
    z, sub = ids[1], ids[2]
    size = rh.shape[1]
    cut = SLAB // 2
    quarter = kept_rows.shape[0] // 4

    def keep(source, place):
        for core in range(2):
            first = z * SLAB + (2 * sub + core) * quarter
            kept_rows[pl.ds((2 * core + place) * quarter, quarter), :] = source[
                pl.ds(pl.multiple_of(first, quarter), quarter), :
            ]


    def at(k):
        return pl.ds(pl.multiple_of(lax.rem(k, slabs) * SLAB, SLAB), SLAB)

    diagonal = eye_tile((SLAB, SLAB), 0, 0)
    trace = jnp.float32(0)
    for k in range(slabs):
        q = slab(ids, k)
        for d in range(DISTANCES):
            cols = slice(d * SLAB, (d + 1) * SLAB)
            block = jnp.concatenate([pieces[2 * k][:, cols], pieces[2 * k + 1][:, cols]], 0)
            y[at(q), at(q + d)] = block
            if d == 0:
                trace += jnp.sum(jnp.where(diagonal, block + damping, 0.0))
            elif d < DISTANCES - 1:
                y[at(q + d), at(q)] = block.T
    keep(y, 0)
    norm = 2.0 * trace / size
    inverse = 1.0 / norm

    def fill_y(rows, i):
        eye = eye_tile((TILE, size), i * TILE, 0)
        v = (y[rows, :] + jnp.where(eye, damping, 0.0)) * inverse
        y[rows, :] = v
        yh[rows, :], yl[rows, :] = halves(v)

    tiles(size // TILE, fill_y)

    half = size // 2

    def fill_z(cols, j):
        for_halves(lambda rows, i: fill_z_half(rows, cols, i, j), half)

    def fill_z_half(rows, cols, i, j):
        eye = eye_tile((half, TILE), i * half, j * TILE)
        v = dot(yh[rows, :], yh[:, cols]) + (
            dot(yh[rows, :], yl[:, cols]) + dot(yl[rows, :], yh[:, cols])
        )
        zh[rows, cols], zl[rows, cols] = halves(v)
        q = jnp.where(eye, 1.6875, 0.0) - 0.5625 * y[rows, cols] + 0.0625 * v
        qh[rows, cols], ql[rows, cols] = halves(q)

    tiles(size // TILE, fill_z)
    scale = lax.rsqrt(jnp.full((1, 1), norm, f32))

    def fill_root(cols, j):
        for_halves(lambda rows, i: fill_root_half(rows, cols, i, j), half)

    def fill_root_half(rows, cols, i, j):
        eye = eye_tile((half, TILE), i * half, j * TILE)
        v = dot(zh[rows, :], qh[:, cols]) + (
            dot(zh[rows, :], ql[:, cols]) + dot(zl[rows, :], qh[:, cols])
        )
        v = (jnp.where(eye, 2.25, 0.0) - 2.4375 * y[rows, cols] + v) * scale
        root[rows, cols] = v
        rh[rows, cols] = v.astype(bf16)

    tiles(size // TILE, fill_root)
    keep(root, 1)
    acc = jnp.zeros((SLAB, size), f32)
    for d in range(DISTANCES):
        cols = slice(d * SLAB, (d + 1) * SLAB)
        weight = 2.0 if 0 < d < DISTANCES - 1 else 1.0
        high, low = halves(jnp.concatenate([part_a[:, cols], part_b[:, cols]], 0) * weight)
        acc += dot(high, rh[at(z + d), :]) + dot(low, rh[at(z + d), :])
    total = jnp.sum(acc * rh[at(z), :].astype(f32))
    lane = lax.broadcasted_iota(jnp.int32, squares.shape, 2)
    squares[...] = jnp.where(lane == 0, gsq[0, 0], jnp.where(lane == 1, total, 0.0))


def root(ids, gsq, pieces, part, size, rows, peers):
    square = lambda kind: pltpu.VMEM((size, size), kind)
    return call(
        root_kernel,
        [((size, size), bf16), ((rows, size), f32), ((peers, 1, 128), f32)],
        [held((size, size)), held((rows, size)), held((peers, 1, 128))],
        [scalar()] + [held(PIECE)] * (len(pieces) + 2),
        [square(f32)] + [square(bf16)] * 6 + [square(f32)],
        40,
        2 * size**3 * 6,
        "root",
    )(ids, gsq, *pieces, *part)


def product_kernel(ids, wide, rh, own, other):
    size = rh.shape[0]
    half = size // 2
    for out, who in ((own, ids[0]), (other, 1 - ids[0])):
        rows = pl.ds(pl.multiple_of(who * half, half), half)

        def fill(cols, j):
            out[:, cols] = dot(wide[rows, :size], rh[:, cols])

        tiles(size // TILE, fill)


def product(ids, wide, rh):
    size = rh.shape[0]
    return call(
        product_kernel,
        [((size // 2, size), f32)] * 2,
        [held((size // 2, size))] * 2,
        [held(wide.shape), held(rh.shape)],
        [],
        16,
        2 * size**3,
        "product",
    )(ids, wide, rh)


def finish_kernel(ids, squares, own, other, update, kept):
    size = own.shape[1]

    @pl.when(pl.program_id(0) == 0)
    def _():
        sums = jnp.sum(squares[...], axis=0)
        kept[...] = jnp.broadcast_to(
            jnp.sqrt(sums[:, 0:1] / (sums[:, 1:2] + epsilon)), kept.shape
        )

    scale = kept[0:1, 0:1]
    for block, who in ((own, ids[0]), (other, 1 - ids[0])):
        cols = pl.ds(pl.multiple_of(who * size, size), size)
        update[:, cols] = (block[...] * scale).astype(update.dtype)


def finish(ids, squares, own, other):
    rows, size = own.shape
    return pl.pallas_call(
        finish_kernel,
        out_shape=jax.ShapeDtypeStruct((rows, 2 * size), bf16),
        grid_spec=pltpu.PrefetchScalarGridSpec(
            num_scalar_prefetch=1,
            grid=(rows // SLAB,),
            in_specs=[
                pl.BlockSpec(squares.shape, lambda i, s: (0, 0, 0)),
                pl.BlockSpec((SLAB, size), lambda i, s: (i, 0)),
                pl.BlockSpec((SLAB, size), lambda i, s: (i, 0)),
            ],
            out_specs=pl.BlockSpec((SLAB, 2 * size), lambda i, s: (i, 0)),
            scratch_shapes=[pltpu.VMEM((8, 128), f32)],
        ),
        compiler_params=pltpu.CompilerParams(vmem_limit_bytes=16 << 20),
        name="finish",
    )(ids, squares, own, other)


def shift(x, by):
    count = lax.axis_size("z")
    return lax.ppermute(x, "z", [(i, (i + by) % count) for i in range(count)])


def swap(x, axis):
    return lax.ppermute(x, axis, [(0, 1), (1, 0)])


def by_index(which, mine, other, dim):
    return jnp.where(
        which == 0, jnp.concatenate([mine, other], dim), jnp.concatenate([other, mine], dim)
    )


def chip_stats(col_stats, core, z, size):
    rows = col_stats.shape[0]
    mine = lax.dynamic_slice_in_dim(col_stats, core * size, size, 1)
    theirs = lax.dynamic_slice_in_dim(col_stats, (1 - core) * size, size, 1)
    chip = by_index(core, mine, swap(theirs, "core"), 0)
    wide = jnp.concatenate([chip, chip[:, : (DISTANCES - 1) * SLAB]], 1)
    return lax.dynamic_slice(wide, (0, z * SLAB), (2 * rows, DISTANCES * SLAB))


def reduce_ring(pieces):
    def chain(h, first, by):
        sum_ = shift(pieces[2 * first + h], by)
        for k in range(first - by, 0 if by > 0 else 8, -by):
            sum_ = shift(pieces[2 * k + h] + sum_, by)
        return sum_

    up_a, down_b = chain(0, 4, 1), chain(1, 4, -1)
    up_b, down_a = chain(1, 3, 1), chain(0, 5, -1)
    return pieces[0] + up_a + down_a, pieces[1] + up_b + down_b


def gather_ring(own):
    pieces = list(own) + [None] * 14
    for hops in range(4):
        for h, by in ((0, 1), (1, -1), (1, 1), (0, -1)):
            if hops == 3 and (h, by) in ((1, 1), (0, -1)):
                continue
            source = -by * hops % 8
            pieces[2 * (-by * (hops + 1) % 8) + h] = shift(pieces[2 * source + h], by)
    return pieces


def exchange_rows(x, core):
    rows = x.shape[0] // 2
    mine = lax.dynamic_slice_in_dim(x, core * rows, rows, 0)
    theirs = lax.dynamic_slice_in_dim(x, (1 - core) * rows, rows, 0)
    return by_index(core, mine, swap(theirs, "core"), 1)


def shards(acts, grads, row_roots, col_stats):
    size = row_roots.shape[1]
    z, sub, core = lax.axis_index("z"), lax.axis_index("yl"), lax.axis_index("core")
    ids = jnp.stack([core, z, sub]).astype(jnp.int32)
    total_rows = grads.shape[1] * lax.axis_size(("z", "yl", "core"))
    mix = (1.0 - decay_rate) / total_rows

    grads_other, roots_other = swap(grads, "core"), swap(row_roots, "core")
    mine = lax.dynamic_slice_in_dim(acts, core * size, size, 1)
    old = decay_rate * chip_stats(col_stats, core, z, size)
    wide, gsq, *pieces = whiten(ids, mine, grads, grads_other, row_roots, roots_other)
    part = reduce_ring(pieces)
    stats = [mix * part[h] + jnp.where(sub == h, old, 0.0) for h in range(2)]
    stats = [x + swap(x, "yl") for x in stats]
    peers = ("z", "yl", "core", "x", "yh")
    rows = col_stats.shape[0]
    half_roots, kept_rows, squares = root(
        ids, gsq, gather_ring(stats), part, size, 4 * rows, lax.axis_size(peers)
    )
    squares = lax.all_to_all(squares, peers, 0, 0, tiled=True)
    own, other = product(ids, wide, half_roots)
    update = finish(ids, squares, own, swap(other, "core"))
    kept_rows = exchange_rows(kept_rows, core)
    return update, kept_rows[:rows], kept_rows[rows:]


def solution(mesh):
    names = ("z", "yl", "core", "x", "yh")
    fine = Mesh(mesh.devices.reshape(8, 2, 2, 4, 2), names)
    row, col = names[:3], names[3:]
    return jax.shard_map(
        shards,
        mesh=fine,
        in_specs=(P(None, col), P(None, row), P(row, None), P(row, col)),
        out_specs=(P(row, col), P(row, col), P(row, col)),
        check_vma=False,
    )
```

profile of v0, /device:TPU:1, one launch (start us, length us, event | category | flops | bytes accessed | tf_op | source)
XLA Modules:
  0.0 155.2 jit_solution(13612490891839518122)
XLA Ops:
  0.6 3.3 %collective-permute-start = (bf16[1024,512]{1,0:T(8,128)(2,1)}, bf16[1024,512]{1,0:T(8,128)(2,1)S(1)}, u32[]{:S(2)}, u32[]{:S(2)}) collective-permute-start(bf16[1024,512]{1,0:T(8,128)(2,1)} %g_own.1), channel_id=1, source_target_pairs={{0,8},{8,0},{1,9},{9,1},{2,10},{10,2},{3,11},{11,3},{4,12},{12,4},... | collective-permute-start | bytes 3145736 | tf_op jit(solution)/shard_map/ppermute | solution.py:310
  4.1 3.2 %constant_dynamic-slice_fusion.4.acts = bf16[1024,1024]{1,0:T(8,128)(2,1)} fusion(bf16[1024,2048]{1,0:T(8,128)(2,1)} %param.4, s32[]{:T(128)S(6)} %select_n.46), kind=kLoop, calls=%fused_computation.14 | loop fusion | bytes 4194308 | tf_op jit(solution)/shard_map/dynamic_slice | solution.py:366
  9.6 14.4 %whiten.1 = (bf16[1024,1536]{1,0:T(8,128)(2,1)}, f32[1,1]{1,0:T(1,128)}, f32[64,640]{1,0:T(8,128)S(1)}, f32[64,640]{1,0:T(8,128)S(1)}, f32[64,640]{1,0:T(8,128)S...) custom-call(s32[3]{0:T(128)S(1)} %pad_add_fusion.ids, ...), custom_call_target="tpu_custom_call" | custom-call | flops 5637144576 | bytes 8388608 | tf_op jit(solution)/shard_map/whiten/pallas_call | solution.py:116
  24.1 3.9 %collective-permute-start.14 = (f32[64,640]{1,0:T(8,128)S(1)}, f32[64,640]{1,0:T(8,128)S(1)}, u32[]{:S(2)}, u32[]{:S(2)}) collective-permute-start(f32[64,640]{1,0:T(8,128)S(1)} %get-tuple-element.42), channel_id=1, source_target_pairs={{0,224},{32,0},{64,32},{96,64},{128,96},{160,128},{192,160},{224,1... | collective-permute-start | bytes 491528 | tf_op jit(solution)/shard_map/ppermute | solution.py:306
  29.5 2.7 %collective-permute-done.2 = f32[64,640]{1,0:T(8,128)S(1)} collective-permute-done((f32[64,640]{1,0:T(8,128)S(1)}, f32[64,640]{1,0:T(8,128)S(1)}, u32[]{:S(2)}, u32[]{:S(2)}) %collective-permute-start.2) | collective-permute-done | bytes 163872 | tf_op jit(solution)/shard_map/ppermute | solution.py:306
  32.3 2.7 %collective-permute-start.15 = (f32[64,640]{1,0:T(8,128)S(1)}, f32[64,640]{1,0:T(8,128)S(1)}, u32[]{:S(2)}, u32[]{:S(2)}) collective-permute-start(f32[64,640]{1,0:T(8,128)S(1)} %add.85), channel_id=1, source_target_pairs={{0,224},{32,0},{64,32},{96,64},{128,96},{160,128},{192,160},{224,1... | collective-permute-start | bytes 491528 | tf_op jit(solution)/shard_map/ppermute | solution.py:306
  35.1 3.1 %collective-permute-start.7 = (f32[64,640]{1,0:T(8,128)S(1)}, f32[64,640]{1,0:T(8,128)S(1)}, u32[]{:S(2)}, u32[]{:S(2)}) collective-permute-start(f32[64,640]{1,0:T(8,128)S(1)} %add.75), channel_id=1, source_target_pairs={{0,224},{32,0},{64,32},{96,64},{128,96},{160,128},{192,160},{224,1... | collective-permute-start | bytes 491528 | tf_op jit(solution)/shard_map/ppermute | solution.py:306
  39.7 2.9 %collective-permute-start.16 = (f32[64,640]{1,0:T(8,128)S(1)}, f32[64,640]{1,0:T(8,128)S(1)}, u32[]{:S(2)}, u32[]{:S(2)}) collective-permute-start(f32[64,640]{1,0:T(8,128)S(1)} %add.86), channel_id=1, source_target_pairs={{0,224},{32,0},{64,32},{96,64},{128,96},{160,128},{192,160},{224,1... | collective-permute-start | bytes 491528 | tf_op jit(solution)/shard_map/ppermute | solution.py:306
  42.6 2.1 %collective-permute-start.9 = (f32[32,1024]{1,0:T(8,128)S(1)}, f32[32,1024]{1,0:T(8,128)S(1)}, u32[]{:S(2)}, u32[]{:S(2)}) collective-permute-start(f32[32,1024]{1,0:T(8,128)S(1)} %get-tuple-element.60), channel_id=1, source_target_pairs={{0,8},{8,0},{1,9},{9,1},{2,10},{10,2},{3,11},{11,3},{4,12},{12,4},... | collective-permute-start | bytes 393224 | tf_op jit(solution)/shard_map/ppermute | solution.py:310
  47.4 2.7 %collective-permute-start.17 = (f32[64,640]{1,0:T(8,128)S(1)}, f32[64,640]{1,0:T(8,128)S(1)}, u32[]{:S(2)}, u32[]{:S(2)}) collective-permute-start(f32[64,640]{1,0:T(8,128)S(1)} %add.87), channel_id=1, source_target_pairs={{0,224},{32,0},{64,32},{96,64},{128,96},{160,128},{192,160},{224,1... | collective-permute-start | bytes 491528 | tf_op jit(solution)/shard_map/ppermute | solution.py:306
  51.0 2.7 %collective-permute-done.5 = f32[64,640]{1,0:T(8,128)S(1)} collective-permute-done((f32[64,640]{1,0:T(8,128)S(1)}, f32[64,640]{1,0:T(8,128)S(1)}, u32[]{:S(2)}, u32[]{:S(2)}) %collective-permute-start.5) | collective-permute-done | bytes 163872 | tf_op jit(solution)/shard_map/ppermute | solution.py:306
  55.4 2.7 %collective-permute-done.18 = f32[64,640]{1,0:T(8,128)S(1)} collective-permute-done((f32[64,640]{1,0:T(8,128)S(1)}, f32[64,640]{1,0:T(8,128)S(1)}, u32[]{:S(2)}, u32[]{:S(2)}) %collective-permute-start.18) | collective-permute-done | bytes 163872 | tf_op jit(solution)/shard_map/ppermute | solution.py:310
  62.1 1.9 %collective-permute-start.19 = (f32[64,640]{1,0:T(8,128)S(1)}, f32[64,640]{1,0:T(8,128)S(1)}, u32[]{:S(2)}, u32[]{:S(2)}) collective-permute-start(f32[64,640]{1,0:T(8,128)S(1)} %add.81.refs_0_), channel_id=1, source_target_pairs={{0,224},{32,0},{64,32},{96,64},{128,96},{160,128},{192,160},{224,1... | collective-permute-start | bytes 491528 | tf_op jit(solution)/shard_map/ppermute | solution.py:306
  64.1 3.4 %collective-permute-start.22 = (f32[64,640]{1,0:T(8,128)S(1)}, f32[64,640]{1,0:T(8,128)S(1)}, u32[]{:S(2)}, u32[]{:S(2)}) collective-permute-start(f32[64,640]{1,0:T(8,128)S(1)} %collective-permute-done.20.refs_3_), channel_id=1, source_target_pairs={{0,224},{32,0},{64,32},{96,64},{128,96},{160,128},{192,160},{224,1... | collective-permute-start | bytes 491528 | tf_op jit(solution)/shard_map/ppermute | solution.py:306
  69.0 4.6 %collective-permute-start.21 = (f32[64,640]{1,0:T(8,128)S(1)}, f32[64,640]{1,0:T(8,128)S(1)}, u32[]{:S(2)}, u32[]{:S(2)}) collective-permute-start(f32[64,640]{1,0:T(8,128)S(1)} %collective-permute-done.19.refs_2_), channel_id=1, source_target_pairs={{0,224},{32,0},{64,32},{96,64},{128,96},{160,128},{192,160},{224,1... | collective-permute-start | bytes 491528 | tf_op jit(solution)/shard_map/ppermute | solution.py:306
  76.9 3.7 %collective-permute-start.23 = (f32[64,640]{1,0:T(8,128)S(1)}, f32[64,640]{1,0:T(8,128)S(1)}, u32[]{:S(2)}, u32[]{:S(2)}) collective-permute-start(f32[64,640]{1,0:T(8,128)S(1)} %collective-permute-done.21.refs_4_), channel_id=1, source_target_pairs={{0,224},{32,0},{64,32},{96,64},{128,96},{160,128},{192,160},{224,1... | collective-permute-start | bytes 491528 | tf_op jit(solution)/shard_map/ppermute | solution.py:306
  82.0 2.0 %collective-permute-done.32.refs_11_ = f32[64,640]{1,0:T(8,128)S(1)} collective-permute-done((f32[64,640]{1,0:T(8,128)S(1)}, f32[64,640]{1,0:T(8,128)S(1)}, u32[]{:S(2)}, u32[]{:S(2)}) %collective-permute-start.32) | collective-permute-done | bytes 163872 | tf_op jit(solution)/shard_map/ppermute | solution.py:306
  86.2 2.1 %collective-permute-done.28.refs_8_ = f32[64,640]{1,0:T(8,128)S(1)} collective-permute-done((f32[64,640]{1,0:T(8,128)S(1)}, f32[64,640]{1,0:T(8,128)S(1)}, u32[]{:S(2)}, u32[]{:S(2)}) %collective-permute-start.28) | collective-permute-done | bytes 163872 | tf_op jit(solution)/shard_map/ppermute | solution.py:306
  88.3 22.0 %root.1 = (bf16[1024,1024]{1,0:T(8,128)(2,1)S(1)}, f32[128,1024]{1,0:T(8,128)S(1)}, f32[256,1,128]{2,1,0:T(1,128)}) custom-call(s32[3]{0:T(128)S(1)} %pad_add_fusion.ids, f32[1,1]{1,0:T(1,128)} %get-tuple-element.26.gsq, f32[64,640]{1,0:T(8,128)S(1)} %add.81.refs_0_, f32[64,640]{1,0:T(8,128)S(1)} %add.90.refs_1_, ...), custom_call_target="tpu_custom_call" | custom-call | flops 12884901888 | bytes 8388608 | tf_op jit(solution)/shard_map/root/pallas_call | solution.py:229
  110.2 5.5 %product.1 = (f32[512,1024]{1,0:T(8,128)S(1)}, f32[512,1024]{1,0:T(8,128)}) custom-call(s32[3]{0:T(128)S(1)} %pad_add_fusion.ids, bf16[1024,1536]{1,0:T(8,128)(2,1)S(1)} %copy-done.4, bf16[1024,1024]{1,0:T(8,128)(2,1)S(1)} %get-tuple-element.45.rh), custom_call_target="tpu_custom_call" | custom-call | flops 2147483648 | bytes 8388608 | tf_op jit(solution)/shard_map/product/pallas_call | solution.py:255
  115.8 6.6 %collective-permute-start.33 = (f32[512,1024]{1,0:T(8,128)}, f32[512,1024]{1,0:T(8,128)}, u32[]{:S(2)}, u32[]{:S(2)}) collective-permute-start(f32[512,1024]{1,0:T(8,128)} %get-tuple-element.47), channel_id=1, source_target_pairs={{0,8},{8,0},{1,9},{9,1},{2,10},{10,2},{3,11},{11,3},{4,12},{12,4},... | collective-permute-start | bytes 6291464 | tf_op jit(solution)/shard_map/ppermute | solution.py:310
  122.6 14.7 %all-to-all-start = ((f32[256,1,128]{2,1,0:T(1,128)}), f32[256,1,128]{2,1,0:T(1,128)S(1)}, u32[]{:S(2)}, u32[]{:S(2)}) async-start(f32[256,1,128]{2,1,0:T(1,128)} %get-tuple-element.43), calls=%async_computation | async-start | bytes 262144 | tf_op jit(solution)/shard_map/all_to_all | solution.py:377
  138.1 12.2 %all-to-all-done.squares = f32[256,1,128]{2,1,0:T(1,128)S(1)} async-done(((f32[256,1,128]{2,1,0:T(1,128)}), f32[256,1,128]{2,1,0:T(1,128)S(1)}, u32[]{:S(2)}, u32[]{:S(2)}) %all-to-all-start) | async-done | bytes 131104 | tf_op jit(solution)/shard_map/all_to_all | solution.py:377
  150.3 4.9 %finish.1 = bf16[512,2048]{1,0:T(8,128)(2,1)} custom-call(s32[3]{0:T(128)S(1)} %pad_add_fusion.ids, f32[256,1,128]{2,1,0:T(1,128)S(1)} %all-to-all-done.squares, f32[512,1024]{1,0:T(8,128)S(1)} %get-tuple-element.46.own, f32[512,1024]{1,0:T(8,128)} %collective-permute-done.33.other), custom_call_target="tpu_custom_call" | custom-call | tf_op jit(solution)/shard_map/finish/pallas_call | solution.py:285
  (85 shorter events, 24.3 us)
Async XLA Ops:
  24.0 8.1 %collective-permute-start.2 = (f32[64,640]{1,0:T(8,128)S(1)}, f32[64,640]{1,0:T(8,128)S(1)}, u32[]{:S(2)}, u32[]{:S(2)}) collective-permute-start(f32[64,640]{1,0:T(8,128)S(1)} %get-tuple-element.31), channel_id=1, source_target_pairs={{0,32},{32,64},{64,96},{96,128},{128,160},{160,192},{192,224},{224... | collective-permute-start | bytes 491528 | tf_op jit(solution)/shard_map/ppermute | solution.py:306
  24.1 8.2 %collective-permute-start.14 = (f32[64,640]{1,0:T(8,128)S(1)}, f32[64,640]{1,0:T(8,128)S(1)}, u32[]{:S(2)}, u32[]{:S(2)}) collective-permute-start(f32[64,640]{1,0:T(8,128)S(1)} %get-tuple-element.42), channel_id=1, source_target_pairs={{0,224},{32,0},{64,32},{96,64},{128,96},{160,128},{192,160},{224,1... | collective-permute-start | bytes 491528 | tf_op jit(solution)/shard_map/ppermute | solution.py:306
  28.0 7.0 %collective-permute-start.6 = (f32[64,640]{1,0:T(8,128)S(1)}, f32[64,640]{1,0:T(8,128)S(1)}, u32[]{:S(2)}, u32[]{:S(2)}) collective-permute-start(f32[64,640]{1,0:T(8,128)S(1)} %get-tuple-element.34), channel_id=1, source_target_pairs={{0,224},{32,0},{64,32},{96,64},{128,96},{160,128},{192,160},{224,1... | collective-permute-start | bytes 491528 | tf_op jit(solution)/shard_map/ppermute | solution.py:306
  29.4 8.8 %collective-permute-start.11 = (f32[64,640]{1,0:T(8,128)S(1)}, f32[64,640]{1,0:T(8,128)S(1)}, u32[]{:S(2)}, u32[]{:S(2)}) collective-permute-start(f32[64,640]{1,0:T(8,128)S(1)} %get-tuple-element.38), channel_id=1, source_target_pairs={{0,32},{32,64},{64,96},{96,128},{128,160},{160,192},{192,224},{224... | collective-permute-start | bytes 491528 | tf_op jit(solution)/shard_map/ppermute | solution.py:306
  32.2 7.4 %collective-permute-start.3 = (f32[64,640]{1,0:T(8,128)S(1)}, f32[64,640]{1,0:T(8,128)S(1)}, u32[]{:S(2)}, u32[]{:S(2)}) collective-permute-start(f32[64,640]{1,0:T(8,128)S(1)} %add.71), channel_id=1, source_target_pairs={{0,32},{32,64},{64,96},{96,128},{128,160},{160,192},{192,224},{224... | collective-permute-start | bytes 491528 | tf_op jit(solution)/shard_map/ppermute | solution.py:306
  32.3 7.4 %collective-permute-start.15 = (f32[64,640]{1,0:T(8,128)S(1)}, f32[64,640]{1,0:T(8,128)S(1)}, u32[]{:S(2)}, u32[]{:S(2)}) collective-permute-start(f32[64,640]{1,0:T(8,128)S(1)} %add.85), channel_id=1, source_target_pairs={{0,224},{32,0},{64,32},{96,64},{128,96},{160,128},{192,160},{224,1... | collective-permute-start | bytes 491528 | tf_op jit(solution)/shard_map/ppermute | solution.py:306
  35.1 9.7 %collective-permute-start.7 = (f32[64,640]{1,0:T(8,128)S(1)}, f32[64,640]{1,0:T(8,128)S(1)}, u32[]{:S(2)}, u32[]{:S(2)}) collective-permute-start(f32[64,640]{1,0:T(8,128)S(1)} %add.75), channel_id=1, source_target_pairs={{0,224},{32,0},{64,32},{96,64},{128,96},{160,128},{192,160},{224,1... | collective-permute-start | bytes 491528 | tf_op jit(solution)/shard_map/ppermute | solution.py:306
  38.3 7.3 %collective-permute-start.12 = (f32[64,640]{1,0:T(8,128)S(1)}, f32[64,640]{1,0:T(8,128)S(1)}, u32[]{:S(2)}, u32[]{:S(2)}) collective-permute-start(f32[64,640]{1,0:T(8,128)S(1)} %add.82), channel_id=1, source_target_pairs={{0,32},{32,64},{64,96},{96,128},{128,160},{160,192},{192,224},{224... | collective-permute-start | bytes 491528 | tf_op jit(solution)/shard_map/ppermute | solution.py:306
  39.6 7.6 %collective-permute-start.4 = (f32[64,640]{1,0:T(8,128)S(1)}, f32[64,640]{1,0:T(8,128)S(1)}, u32[]{:S(2)}, u32[]{:S(2)}) collective-permute-start(f32[64,640]{1,0:T(8,128)S(1)} %add.72), channel_id=1, source_target_pairs={{0,32},{32,64},{64,96},{96,128},{128,160},{160,192},{192,224},{224... | collective-permute-start | bytes 491528 | tf_op jit(solution)/shard_map/ppermute | solution.py:306
  39.7 7.6 %collective-permute-start.16 = (f32[64,640]{1,0:T(8,128)S(1)}, f32[64,640]{1,0:T(8,128)S(1)}, u32[]{:S(2)}, u32[]{:S(2)}) collective-permute-start(f32[64,640]{1,0:T(8,128)S(1)} %add.86), channel_id=1, source_target_pairs={{0,224},{32,0},{64,32},{96,64},{128,96},{160,128},{192,160},{224,1... | collective-permute-start | bytes 491528 | tf_op jit(solution)/shard_map/ppermute | solution.py:306
  42.6 7.5 %collective-permute-start.9 = (f32[32,1024]{1,0:T(8,128)S(1)}, f32[32,1024]{1,0:T(8,128)S(1)}, u32[]{:S(2)}, u32[]{:S(2)}) collective-permute-start(f32[32,1024]{1,0:T(8,128)S(1)} %get-tuple-element.60), channel_id=1, source_target_pairs={{0,8},{8,0},{1,9},{9,1},{2,10},{10,2},{3,11},{11,3},{4,12},{12,4},... | collective-permute-start | bytes 393224 | tf_op jit(solution)/shard_map/ppermute | solution.py:310
  60.0 7.5 %collective-permute-start.25 = (f32[64,640]{1,0:T(8,128)S(1)}, f32[64,640]{1,0:T(8,128)S(1)}, u32[]{:S(2)}, u32[]{:S(2)}) collective-permute-start(f32[64,640]{1,0:T(8,128)S(1)} %add.81.refs_0_), channel_id=1, source_target_pairs={{0,32},{32,64},{64,96},{96,128},{128,160},{160,192},{192,224},{224... | collective-permute-start | bytes 491528 | tf_op jit(solution)/shard_map/ppermute | solution.py:306
  60.6 7.8 %collective-permute-start.30 = (f32[64,640]{1,0:T(8,128)S(1)}, f32[64,640]{1,0:T(8,128)S(1)}, u32[]{:S(2)}, u32[]{:S(2)}) collective-permute-start(f32[64,640]{1,0:T(8,128)S(1)} %add.90.refs_1_), channel_id=1, source_target_pairs={{0,32},{32,64},{64,96},{96,128},{128,160},{160,192},{192,224},{224... | collective-permute-start | bytes 491528 | tf_op jit(solution)/shard_map/ppermute | solution.py:306
  64.1 9.6 %collective-permute-start.22 = (f32[64,640]{1,0:T(8,128)S(1)}, f32[64,640]{1,0:T(8,128)S(1)}, u32[]{:S(2)}, u32[]{:S(2)}) collective-permute-start(f32[64,640]{1,0:T(8,128)S(1)} %collective-permute-done.20.refs_3_), channel_id=1, source_target_pairs={{0,224},{32,0},{64,32},{96,64},{128,96},{160,128},{192,160},{224,1... | collective-permute-start | bytes 491528 | tf_op jit(solution)/shard_map/ppermute | solution.py:306
  67.5 7.6 %collective-permute-start.26 = (f32[64,640]{1,0:T(8,128)S(1)}, f32[64,640]{1,0:T(8,128)S(1)}, u32[]{:S(2)}, u32[]{:S(2)}) collective-permute-start(f32[64,640]{1,0:T(8,128)S(1)} %collective-permute-done.25.refs_14_), channel_id=1, source_target_pairs={{0,32},{32,64},{64,96},{96,128},{128,160},{160,192},{192,224},{224... | collective-permute-start | bytes 491528 | tf_op jit(solution)/shard_map/ppermute | solution.py:306
  68.3 8.5 %collective-permute-start.31 = (f32[64,640]{1,0:T(8,128)S(1)}, f32[64,640]{1,0:T(8,128)S(1)}, u32[]{:S(2)}, u32[]{:S(2)}) collective-permute-start(f32[64,640]{1,0:T(8,128)S(1)} %collective-permute-done.30.refs_15_), channel_id=1, source_target_pairs={{0,32},{32,64},{64,96},{96,128},{128,160},{160,192},{192,224},{224... | collective-permute-start | bytes 491528 | tf_op jit(solution)/shard_map/ppermute | solution.py:306
  69.0 7.8 %collective-permute-start.21 = (f32[64,640]{1,0:T(8,128)S(1)}, f32[64,640]{1,0:T(8,128)S(1)}, u32[]{:S(2)}, u32[]{:S(2)}) collective-permute-start(f32[64,640]{1,0:T(8,128)S(1)} %collective-permute-done.19.refs_2_), channel_id=1, source_target_pairs={{0,224},{32,0},{64,32},{96,64},{128,96},{160,128},{192,160},{224,1... | collective-permute-start | bytes 491528 | tf_op jit(solution)/shard_map/ppermute | solution.py:306
  73.6 6.9 %collective-permute-start.24 = (f32[64,640]{1,0:T(8,128)S(1)}, f32[64,640]{1,0:T(8,128)S(1)}, u32[]{:S(2)}, u32[]{:S(2)}) collective-permute-start(f32[64,640]{1,0:T(8,128)S(1)} %collective-permute-done.22.refs_5_), channel_id=1, source_target_pairs={{0,224},{32,0},{64,32},{96,64},{128,96},{160,128},{192,160},{224,1... | collective-permute-start | bytes 491528 | tf_op jit(solution)/shard_map/ppermute | solution.py:306
  75.1 6.9 %collective-permute-start.27 = (f32[64,640]{1,0:T(8,128)S(1)}, f32[64,640]{1,0:T(8,128)S(1)}, u32[]{:S(2)}, u32[]{:S(2)}) collective-permute-start(f32[64,640]{1,0:T(8,128)S(1)} %collective-permute-done.26.refs_12_), channel_id=1, source_target_pairs={{0,32},{32,64},{64,96},{96,128},{128,160},{160,192},{192,224},{224... | collective-permute-start | bytes 491528 | tf_op jit(solution)/shard_map/ppermute | solution.py:306
  76.9 7.1 %collective-permute-start.32 = (f32[64,640]{1,0:T(8,128)S(1)}, f32[64,640]{1,0:T(8,128)S(1)}, u32[]{:S(2)}, u32[]{:S(2)}) collective-permute-start(f32[64,640]{1,0:T(8,128)S(1)} %collective-permute-done.31.refs_13_), channel_id=1, source_target_pairs={{0,32},{32,64},{64,96},{96,128},{128,160},{160,192},{192,224},{224... | collective-permute-start | bytes 491528 | tf_op jit(solution)/shard_map/ppermute | solution.py:306
  76.9 7.6 %collective-permute-start.23 = (f32[64,640]{1,0:T(8,128)S(1)}, f32[64,640]{1,0:T(8,128)S(1)}, u32[]{:S(2)}, u32[]{:S(2)}) collective-permute-start(f32[64,640]{1,0:T(8,128)S(1)} %collective-permute-done.21.refs_4_), channel_id=1, source_target_pairs={{0,224},{32,0},{64,32},{96,64},{128,96},{160,128},{192,160},{224,1... | collective-permute-start | bytes 491528 | tf_op jit(solution)/shard_map/ppermute | solution.py:306
  115.8 34.5 %collective-permute-start.33 = (f32[512,1024]{1,0:T(8,128)}, f32[512,1024]{1,0:T(8,128)}, u32[]{:S(2)}, u32[]{:S(2)}) collective-permute-start(f32[512,1024]{1,0:T(8,128)} %get-tuple-element.47), channel_id=1, source_target_pairs={{0,8},{8,0},{1,9},{9,1},{2,10},{10,2},{3,11},{11,3},{4,12},{12,4},... | collective-permute-start | bytes 6291464 | tf_op jit(solution)/shard_map/ppermute | solution.py:310
  122.5 14.8 %collective-permute-start.34 = (f32[64,1024]{1,0:T(8,128)S(1)}, f32[64,1024]{1,0:T(8,128)S(1)}, u32[]{:S(2)}, u32[]{:S(2)}) collective-permute-start(f32[64,1024]{1,0:T(8,128)S(1)} %get-tuple-element.56), channel_id=1, source_target_pairs={{0,8},{8,0},{1,9},{9,1},{2,10},{10,2},{3,11},{11,3},{4,12},{12,4},... | collective-permute-start | bytes 786440 | tf_op jit(solution)/shard_map/ppermute | solution.py:310
  122.6 27.7 %all-to-all-start = ((f32[256,1,128]{2,1,0:T(1,128)}), f32[256,1,128]{2,1,0:T(1,128)S(1)}, u32[]{:S(2)}, u32[]{:S(2)}) async-start(f32[256,1,128]{2,1,0:T(1,128)} %get-tuple-element.43), calls=%async_computation | async-start | bytes 262144 | tf_op jit(solution)/shard_map/all_to_all | solution.py:377
  (18 other events, 120.4 us)
where the time goes:
time: 155 us
  starting transfers between devices  68 us (44%)
  Pallas kernels  46.8 us (30%)
  waiting for transfers between devices  32.7 us (21%)
  local copies, waits for them, and re-layouts  6.36 us (4%)
    ppermute x28, starting transfers between devices, shift(): return lax.ppermute(x, 'z', [(i, (i + by) % count) for i in range(count)])  39.5 us
    pallas_call x1, Pallas kernels, root(): call(root_kernel, [((size, size), bf16), ((rows, size), f32), ((peers, 1,...  22 us
    ppermute x28, waiting for transfers between devices, shift(): return lax.ppermute(x, 'z', [(i, (i + by) % count) for i in range(count)])  17.8 us
    all_to_all x1, starting transfers between devices, shards(): squares = lax.all_to_all(squares, peers, 0, 0, tiled=True)  14.7 us
    pallas_call x1, Pallas kernels, whiten(): call(whiten_kernel, [(wide, bf16), ((1, 1), f32)] + [(PIECE, f32)] * coun...  14.4 us
    ppermute x7, starting transfers between devices, swap(): return lax.ppermute(x, axis, [(0, 1), (1, 0)])  13.9 us
    all_to_all x1, waiting for transfers between devices, shards(): squares = lax.all_to_all(squares, peers, 0, 0, tiled=True)  12.2 us
    pallas_call x1, Pallas kernels, product(): call(product_kernel, [((size // 2, size), f32)] * 2, [held((size // 2, si...  5.53 us
  transfers between devices with their start and end apart: 36, of which 15 were waited for; matrix products, arithmetic and copies ran while one was open for 3% of the time, Pallas kernels for 0%

commit v1 on v0

--- a/solution.py
+++ b/solution.py
@@ -69,31 +69,48 @@
     return lax.rem(ids[1] + k, 8)
 
 
-def fill_grad(g, acts, grad, first, gsq):
-    half = g.shape[1]
-
-    def fill(cols, j):
-        t = tdot(g[...], acts[:, cols]).astype(bf16)
-        grad[pl.ds(first, half), cols] = t
-        gsq[0, 0] += jnp.sum(jnp.square(t.astype(f32)))
-
-    tiles(acts.shape[1] // TILE, fill)
-
-
 def whiten_kernel(ids, acts, g_own, g_other, r_own, r_other, wide, gsq, *rest):
-    pieces, grad = rest[:-1], rest[-1]
+    pieces, (block, g, r, grad, tile_sems, sems) = rest[:-6], rest[-6:]
     core = ids[0]
     half = g_own.shape[1]
-    size = acts.shape[1]
+    size = block.shape[1]
     cut = SLAB // 2
+
+    def tile_copy(j):
+        source = pl.ds(pl.multiple_of(core * size + j * TILE, TILE), TILE)
+        target = pl.ds(pl.multiple_of(j * TILE, TILE), TILE)
+        return pltpu.make_async_copy(acts.at[:, source], block.at[:, target], tile_sems.at[j])
+
+    copies = [
+        pltpu.make_async_copy(source, target, sems.at[i])
+        for i, (source, target) in enumerate(
+            ((g_own, g.at[0]), (g_other, g.at[1]), (r_own, r.at[0]), (r_other, r.at[1]))
+        )
+    ]
+    copies[0].start()
+    for j in range(size // TILE):
+        tile_copy(j).start()
+    for copy in copies[1:]:
+        copy.start()
     gsq[0, 0] = 0.0
-    for g, who in ((g_own, core), (g_other, 1 - core)):
-        fill_grad(g, acts, grad, pl.multiple_of(who * half, half), gsq)
-    for r, who in ((r_own, core), (r_other, 1 - core)):
+    for i, who in enumerate((core, 1 - core)):
         first = pl.multiple_of(who * half, half)
+        copies[i].wait()
+
+        def fill_grad(cols, j):
+            if i == 0:
+                tile_copy(j).wait()
+            t = tdot(g[i], block[:, cols]).astype(bf16)
+            grad[pl.ds(first, half), cols] = t
+            gsq[0, 0] += jnp.sum(jnp.square(t.astype(f32)))
+
+        tiles(size // TILE, fill_grad)
+    for i, who in enumerate((core, 1 - core)):
+        first = pl.multiple_of(who * half, half)
+        copies[2 + i].wait()
 
         def fill_white(cols, j):
-            wide[pl.ds(first, half), cols] = dot(r[...], grad[:, cols]).astype(bf16)
+            wide[pl.ds(first, half), cols] = dot(r[i], grad[:, cols]).astype(bf16)
 
         tiles(size // TILE, fill_white)
     wide[:, size:] = wide[:, : (DISTANCES - 1) * SLAB]
@@ -104,21 +121,28 @@
         pieces[2 * k + 1][...] = t[cut:]
 
 
-WHITEN_MIB = 48
+WHITEN_MIB = 52
 PIECE = (SLAB // 2, DISTANCES * SLAB)
 
 
 def whiten(ids, acts, g_own, g_other, r_own, r_other):
     tok, half = g_own.shape
-    size = acts.shape[1]
+    size = r_own.shape[1]
     count = 2 * size // SLAB
     wide = (size, size + (DISTANCES - 1) * SLAB)
     return call(
         whiten_kernel,
         [(wide, bf16), ((1, 1), f32)] + [(PIECE, f32)] * count,
         [held(wide), scalar()] + [held(PIECE)] * count,
-        [held((tok, size))] + [held((tok, half))] * 2 + [held((half, size))] * 2,
-        [pltpu.VMEM((size, size), bf16)],
+        [pl.BlockSpec(memory_space=pl.ANY)] * 5,
+        [
+            pltpu.VMEM((tok, size), bf16),
+            pltpu.VMEM((2, tok, half), bf16),
+            pltpu.VMEM((2, half, size), bf16),
+            pltpu.VMEM((size, size), bf16),
+            pltpu.SemaphoreType.DMA((size // TILE,)),
+            pltpu.SemaphoreType.DMA((4,)),
+        ],
         WHITEN_MIB,
         2 * size * size * (tok + size + DISTANCES * SLAB),
         "whiten",
@@ -140,8 +164,10 @@
 def root_kernel(ids, gsq, *refs):
     slabs = 8
     pieces = refs[: 2 * slabs]
-    part_a, part_b, rh, kept_rows, squares = refs[2 * slabs : 2 * slabs + 5]
-    y, yh, yl, zh, zl, qh, ql, root = refs[2 * slabs + 5 :]
+    part_a, part_b, wide, own, other, kept_rows, squares = refs[2 * slabs : 2 * slabs + 7]
+    y, yh, yl, zh, zl, qh, ql, rh, root, white, white_sem = refs[2 * slabs + 7 :]
+    white_copy = pltpu.make_async_copy(wide.at[:, pl.ds(0, rh.shape[1])], white, white_sem.at[0])
+    white_copy.start()
     z, sub = ids[1], ids[2]
     size = rh.shape[1]
     cut = SLAB // 2
@@ -222,46 +248,31 @@
     total = jnp.sum(acc * rh[at(z), :].astype(f32))
     lane = lax.broadcasted_iota(jnp.int32, squares.shape, 2)
     squares[...] = jnp.where(lane == 0, gsq[0, 0], jnp.where(lane == 1, total, 0.0))
-
-
-def root(ids, gsq, pieces, part, size, rows, peers):
+    white_copy.wait()
+    for out, who in ((own, ids[0]), (other, 1 - ids[0])):
+        rows = pl.ds(pl.multiple_of(who * half, half), half)
+
+        def fill(cols, j):
+            out[:, cols] = dot(white[rows, :], rh[:, cols])
+
+        tiles(size // TILE, fill)
+
+
+def root(ids, gsq, pieces, part, wide, rows, peers):
+    size = wide.shape[0]
     square = lambda kind: pltpu.VMEM((size, size), kind)
     return call(
         root_kernel,
-        [((size, size), bf16), ((rows, size), f32), ((peers, 1, 128), f32)],
-        [held((size, size)), held((rows, size)), held((peers, 1, 128))],
-        [scalar()] + [held(PIECE)] * (len(pieces) + 2),
-        [square(f32)] + [square(bf16)] * 6 + [square(f32)],
-        40,
-        2 * size**3 * 6,
+        [((size // 2, size), f32)] * 2 + [((rows, size), f32), ((peers, 1, 128), f32)],
+        [held((size // 2, size))] * 2 + [held((rows, size)), held((peers, 1, 128))],
+        [scalar()] + [held(PIECE)] * (len(pieces) + 2) + [pl.BlockSpec(memory_space=pl.ANY)],
+        [square(f32)]
+        + [square(bf16)] * 7
+        + [square(f32), square(bf16), pltpu.SemaphoreType.DMA((1,))],
+        44,
+        2 * size**3 * 7,
         "root",
-    )(ids, gsq, *pieces, *part)
-
-
-def product_kernel(ids, wide, rh, own, other):
-    size = rh.shape[0]
-    half = size // 2
-    for out, who in ((own, ids[0]), (other, 1 - ids[0])):
-        rows = pl.ds(pl.multiple_of(who * half, half), half)
-
-        def fill(cols, j):
-            out[:, cols] = dot(wide[rows, :size], rh[:, cols])
-
-        tiles(size // TILE, fill)
-
-
-def product(ids, wide, rh):
-    size = rh.shape[0]
-    return call(
-        product_kernel,
-        [((size // 2, size), f32)] * 2,
-        [held((size // 2, size))] * 2,
-        [held(wide.shape), held(rh.shape)],
-        [],
-        16,
-        2 * size**3,
-        "product",
-    )(ids, wide, rh)
+    )(ids, gsq, *pieces, *part, wide)
 
 
 def finish_kernel(ids, squares, own, other, update, kept):
@@ -363,19 +374,17 @@
     mix = (1.0 - decay_rate) / total_rows
 
     grads_other, roots_other = swap(grads, "core"), swap(row_roots, "core")
-    mine = lax.dynamic_slice_in_dim(acts, core * size, size, 1)
     old = decay_rate * chip_stats(col_stats, core, z, size)
-    wide, gsq, *pieces = whiten(ids, mine, grads, grads_other, row_roots, roots_other)
+    wide, gsq, *pieces = whiten(ids, acts, grads, grads_other, row_roots, roots_other)
     part = reduce_ring(pieces)
     stats = [mix * part[h] + jnp.where(sub == h, old, 0.0) for h in range(2)]
     stats = [x + swap(x, "yl") for x in stats]
     peers = ("z", "yl", "core", "x", "yh")
     rows = col_stats.shape[0]
-    half_roots, kept_rows, squares = root(
-        ids, gsq, gather_ring(stats), part, size, 4 * rows, lax.axis_size(peers)
+    own, other, kept_rows, squares = root(
+        ids, gsq, gather_ring(stats), part, wide, 4 * rows, lax.axis_size(peers)
     )
     squares = lax.all_to_all(squares, peers, 0, 0, tiled=True)
-    own, other = product(ids, wide, half_roots)
     update = finish(ids, squares, own, swap(other, "core"))
     kept_rows = exchange_rows(kept_rows, core)
     return update, kept_rows[:rows], kept_rows[rows:]

time: 155 us -> 152 us (0.981)
  waiting for transfers between devices: 32.7 us -> 39.4 us
  local copies, waits for them, and re-layouts: 6.36 us -> 0.92 us
  starting transfers between devices: 68 us -> 64.4 us
  Pallas kernels: 46.8 us -> 44.5 us
    ppermute x28, starting transfers between devices: 39.5 us -> 34.3 us  [shift(): return lax.ppermute(x, 'z', [(i, (i + by) % count) for i in range(count)])]
    ppermute x7, starting transfers between devices: 13.9 us -> 18.4 us  [swap(): return lax.ppermute(x, axis, [(0, 1), (1, 0)])]
    ppermute x7, waiting for transfers between devices: 2.72 us -> 6.66 us  [swap(): return lax.ppermute(x, axis, [(0, 1), (1, 0)])]
    dynamic_slice x1 -> x0, local copies, waits for them, and re-layouts: 3.23 us -> none  [shards(): mine = lax.dynamic_slice_in_dim(acts, core * size, size, 1)]
    all_to_all x1, starting transfers between devices: 14.7 us -> 11.7 us  [shards(): squares = lax.all_to_all(squares, peers, 0, 0, tiled=True)]
    ppermute x28, waiting for transfers between devices: 17.8 us -> 20.6 us  [shift(): return lax.ppermute(x, 'z', [(i, (i + by) % count) for i in range(count)])]
    unnamed x12 -> x10, local copies, waits for them, and re-layouts: 2.23 us -> 0.02 us
    pallas_call x2 -> x1, Pallas kernels: 27.5 us -> 26.2 us  [root(): call(root_kernel, [((size // 2, size), f32)] * 2 + [((rows, size), f32),...]
  transfers between devices with their start and end apart: 36 -> 36, of which waited for: 15 -> 17; matrix products, arithmetic and copies ran while one was open for 3% -> 1% of each run, Pallas kernels for 0% -> 0%
where the time goes in v1:
time: 152 us; the launch traced here: 151 us
  starting transfers between devices  64.4 us (42%)
  Pallas kernels  44.5 us (29%)
  waiting for transfers between devices  39.4 us (26%)
    ppermute x28, starting transfers between devices, shift(): return lax.ppermute(x, 'z', [(i, (i + by) % count) for i in range(count)])  34.3 us
    pallas_call x1, Pallas kernels, root(): call(root_kernel, [((size // 2, size), f32)] * 2 + [((rows, size), f32),...  26.2 us
    ppermute x28, waiting for transfers between devices, shift(): return lax.ppermute(x, 'z', [(i, (i + by) % count) for i in range(count)])  20.6 us
    ppermute x7, starting transfers between devices, swap(): return lax.ppermute(x, axis, [(0, 1), (1, 0)])  18.4 us
    pallas_call x1, Pallas kernels, whiten(): call(whiten_kernel, [(wide, bf16), ((1, 1), f32)] + [(PIECE, f32)] * coun...  13.3 us
    all_to_all x1, waiting for transfers between devices, shards(): squares = lax.all_to_all(squares, peers, 0, 0, tiled=True)  12.2 us
    all_to_all x1, starting transfers between devices, shards(): squares = lax.all_to_all(squares, peers, 0, 0, tiled=True)  11.7 us
    ppermute x7, waiting for transfers between devices, swap(): return lax.ppermute(x, axis, [(0, 1), (1, 0)])  6.66 us
  transfers between devices with their start and end apart: 36, of which 17 were waited for; matrix products, arithmetic and copies ran while one was open for 1% of the time, Pallas kernels for 0%

profile of v1, /device:TPU:1, one launch (start us, length us, event | category | flops | bytes accessed | tf_op | source)
XLA Modules:
  0.0 151.4 jit_solution(9061772720505697026)
XLA Ops:
  0.6 3.3 %collective-permute-start = (bf16[1024,512]{1,0:T(8,128)(2,1)}, bf16[1024,512]{1,0:T(8,128)(2,1)S(1)}, u32[]{:S(2)}, u32[]{:S(2)}) collective-permute-start(bf16[1024,512]{1,0:T(8,128)(2,1)} %g_own.1), channel_id=1, source_target_pairs={{0,8},{8,0},{1,9},{9,1},{2,10},{10,2},{3,11},{11,3},{4,12},{12,4},... | collective-permute-start | bytes 3145736 | tf_op jit(solution)/shard_map/ppermute | solution.py:321
  4.1 2.8 %collective-permute-done.g_other = bf16[1024,512]{1,0:T(8,128)(2,1)S(1)} collective-permute-done((bf16[1024,512]{1,0:T(8,128)(2,1)}, bf16[1024,512]{1,0:T(8,128)(2,1)S(1)}, u32[]{:S(2)}, u32[]{:S(2)}) %collective-permute-start) | collective-permute-done | bytes 1048608 | tf_op jit(solution)/shard_map/ppermute | solution.py:321
  8.1 13.3 %whiten.1 = (bf16[1024,1536]{1,0:T(8,128)(2,1)}, f32[1,1]{1,0:T(1,128)}, f32[64,640]{1,0:T(8,128)S(1)}, f32[64,640]{1,0:T(8,128)S(1)}, f32[64,640]{1,0:T(8,128)S...) custom-call(s32[3]{0:T(128)S(1)} %pad_add_fusion.ids, ...), custom_call_target="tpu_custom_call" | custom-call | flops 5637144576 | bytes 8388608 | tf_op jit(solution)/shard_map/whiten/pallas_call | solution.py:133
  21.6 3.9 %collective-permute-start.14 = (f32[64,640]{1,0:T(8,128)S(1)}, f32[64,640]{1,0:T(8,128)S(1)}, u32[]{:S(2)}, u32[]{:S(2)}) collective-permute-start(f32[64,640]{1,0:T(8,128)S(1)} %get-tuple-element.41), channel_id=1, source_target_pairs={{0,224},{32,0},{64,32},{96,64},{128,96},{160,128},{192,160},{224,1... | collective-permute-start | bytes 491528 | tf_op jit(solution)/shard_map/ppermute | solution.py:317
  26.9 2.7 %collective-permute-done.2 = f32[64,640]{1,0:T(8,128)S(1)} collective-permute-done((f32[64,640]{1,0:T(8,128)S(1)}, f32[64,640]{1,0:T(8,128)S(1)}, u32[]{:S(2)}, u32[]{:S(2)}) %collective-permute-start.2) | collective-permute-done | bytes 163872 | tf_op jit(solution)/shard_map/ppermute | solution.py:317
  29.8 2.7 %collective-permute-start.15 = (f32[64,640]{1,0:T(8,128)S(1)}, f32[64,640]{1,0:T(8,128)S(1)}, u32[]{:S(2)}, u32[]{:S(2)}) collective-permute-start(f32[64,640]{1,0:T(8,128)S(1)} %add.84), channel_id=1, source_target_pairs={{0,224},{32,0},{64,32},{96,64},{128,96},{160,128},{192,160},{224,1... | collective-permute-start | bytes 491528 | tf_op jit(solution)/shard_map/ppermute | solution.py:317
  33.5 3.1 %collective-permute-start.7 = (f32[64,640]{1,0:T(8,128)S(1)}, f32[64,640]{1,0:T(8,128)S(1)}, u32[]{:S(2)}, u32[]{:S(2)}) collective-permute-start(f32[64,640]{1,0:T(8,128)S(1)} %add.73), channel_id=1, source_target_pairs={{0,224},{32,0},{64,32},{96,64},{128,96},{160,128},{192,160},{224,1... | collective-permute-start | bytes 491528 | tf_op jit(solution)/shard_map/ppermute | solution.py:317
  37.2 2.9 %collective-permute-start.16 = (f32[64,640]{1,0:T(8,128)S(1)}, f32[64,640]{1,0:T(8,128)S(1)}, u32[]{:S(2)}, u32[]{:S(2)}) collective-permute-start(f32[64,640]{1,0:T(8,128)S(1)} %add.85), channel_id=1, source_target_pairs={{0,224},{32,0},{64,32},{96,64},{128,96},{160,128},{192,160},{224,1... | collective-permute-start | bytes 491528 | tf_op jit(solution)/shard_map/ppermute | solution.py:317
  40.1 1.9 %collective-permute-start.9 = (f32[32,1024]{1,0:T(8,128)S(1)}, f32[32,1024]{1,0:T(8,128)S(1)}, u32[]{:S(2)}, u32[]{:S(2)}) collective-permute-start(f32[32,1024]{1,0:T(8,128)S(1)} %get-tuple-element.58), channel_id=1, source_target_pairs={{0,8},{8,0},{1,9},{9,1},{2,10},{10,2},{3,11},{11,3},{4,12},{12,4},... | collective-permute-start | bytes 393224 | tf_op jit(solution)/shard_map/ppermute | solution.py:321
  42.0 1.8 %collective-permute-start.8 = (f32[64,640]{1,0:T(8,128)S(1)}, f32[64,640]{1,0:T(8,128)S(1)}, u32[]{:S(2)}, u32[]{:S(2)}) collective-permute-start(f32[64,640]{1,0:T(8,128)S(1)} %add.74), channel_id=1, source_target_pairs={{0,224},{32,0},{64,32},{96,64},{128,96},{160,128},{192,160},{224,1... | collective-permute-start | bytes 491528 | tf_op jit(solution)/shard_map/ppermute | solution.py:317
  45.8 2.7 %collective-permute-start.17 = (f32[64,640]{1,0:T(8,128)S(1)}, f32[64,640]{1,0:T(8,128)S(1)}, u32[]{:S(2)}, u32[]{:S(2)}) collective-permute-start(f32[64,640]{1,0:T(8,128)S(1)} %add.86), channel_id=1, source_target_pairs={{0,224},{32,0},{64,32},{96,64},{128,96},{160,128},{192,160},{224,1... | collective-permute-start | bytes 491528 | tf_op jit(solution)/shard_map/ppermute | solution.py:317
  49.3 2.8 %collective-permute-done.5 = f32[64,640]{1,0:T(8,128)S(1)} collective-permute-done((f32[64,640]{1,0:T(8,128)S(1)}, f32[64,640]{1,0:T(8,128)S(1)}, u32[]{:S(2)}, u32[]{:S(2)}) %collective-permute-start.5) | collective-permute-done | bytes 163872 | tf_op jit(solution)/shard_map/ppermute | solution.py:317
  53.7 2.7 %collective-permute-done.18 = f32[64,640]{1,0:T(8,128)S(1)} collective-permute-done((f32[64,640]{1,0:T(8,128)S(1)}, f32[64,640]{1,0:T(8,128)S(1)}, u32[]{:S(2)}, u32[]{:S(2)}) %collective-permute-start.18) | collective-permute-done | bytes 163872 | tf_op jit(solution)/shard_map/ppermute | solution.py:321
  56.4 1.9 %collective-permute-start.20 = (f32[64,640]{1,0:T(8,128)S(1)}, f32[64,640]{1,0:T(8,128)S(1)}, u32[]{:S(2)}, u32[]{:S(2)}) collective-permute-start(f32[64,640]{1,0:T(8,128)S(1)} %add.89.refs_1_), channel_id=1, source_target_pairs={{0,224},{32,0},{64,32},{96,64},{128,96},{160,128},{192,160},{224,1... | collective-permute-start | bytes 491528 | tf_op jit(solution)/shard_map/ppermute | solution.py:317
  68.9 2.2 %collective-permute-start.24 = (f32[64,640]{1,0:T(8,128)S(1)}, f32[64,640]{1,0:T(8,128)S(1)}, u32[]{:S(2)}, u32[]{:S(2)}) collective-permute-start(f32[64,640]{1,0:T(8,128)S(1)} %collective-permute-done.22.refs_5_), channel_id=1, source_target_pairs={{0,224},{32,0},{64,32},{96,64},{128,96},{160,128},{192,160},{224,1... | collective-permute-start | bytes 491528 | tf_op jit(solution)/shard_map/ppermute | solution.py:317
  71.1 3.3 %collective-permute-done.31.refs_13_ = f32[64,640]{1,0:T(8,128)S(1)} collective-permute-done((f32[64,640]{1,0:T(8,128)S(1)}, f32[64,640]{1,0:T(8,128)S(1)}, u32[]{:S(2)}, u32[]{:S(2)}) %collective-permute-start.31) | collective-permute-done | bytes 163872 | tf_op jit(solution)/shard_map/ppermute | solution.py:317
  74.5 2.7 %collective-permute-start.23 = (f32[64,640]{1,0:T(8,128)S(1)}, f32[64,640]{1,0:T(8,128)S(1)}, u32[]{:S(2)}, u32[]{:S(2)}) collective-permute-start(f32[64,640]{1,0:T(8,128)S(1)} %collective-permute-done.21.refs_4_), channel_id=1, source_target_pairs={{0,224},{32,0},{64,32},{96,64},{128,96},{160,128},{192,160},{224,1... | collective-permute-start | bytes 491528 | tf_op jit(solution)/shard_map/ppermute | solution.py:317
  78.6 2.4 %collective-permute-done.32.refs_11_ = f32[64,640]{1,0:T(8,128)S(1)} collective-permute-done((f32[64,640]{1,0:T(8,128)S(1)}, f32[64,640]{1,0:T(8,128)S(1)}, u32[]{:S(2)}, u32[]{:S(2)}) %collective-permute-start.32) | collective-permute-done | bytes 163872 | tf_op jit(solution)/shard_map/ppermute | solution.py:317
  81.0 2.2 %collective-permute-done.29.refs_9_ = f32[64,640]{1,0:T(8,128)S(1)} collective-permute-done((f32[64,640]{1,0:T(8,128)S(1)}, f32[64,640]{1,0:T(8,128)S(1)}, u32[]{:S(2)}, u32[]{:S(2)}) %collective-permute-start.29) | collective-permute-done | bytes 163872 | tf_op jit(solution)/shard_map/ppermute | solution.py:317
  84.0 26.2 %root.1 = (f32[512,1024]{1,0:T(8,128)S(1)}, f32[512,1024]{1,0:T(8,128)}, f32[128,1024]{1,0:T(8,128)S(1)}, f32[256,1,128]{2,1,0:T(1,128)}) custom-call(s32[3]{0:T(128)S(1)} %pad_add_fusion.ids, f32[1,1]{1,0:T(1,128)} %get-tuple-element.25.gsq, f32[64,640]{1,0:T(8,128)S(1)} %add.80.refs_0_, f32[64,640]{1,0:T(8,128)S(1)} %add.89.refs_1_, ...), custom_call_target="tpu_custom_call" | custom-call | flops 15032385536 | bytes 8388608 | tf_op jit(solution)/shard_map/root/pallas_call | solution.py:264
  110.2 11.4 %collective-permute-start.33 = (f32[512,1024]{1,0:T(8,128)}, f32[512,1024]{1,0:T(8,128)}, u32[]{:S(2)}, u32[]{:S(2)}) collective-permute-start(f32[512,1024]{1,0:T(8,128)} %get-tuple-element.45), channel_id=1, source_target_pairs={{0,8},{8,0},{1,9},{9,1},{2,10},{10,2},{3,11},{11,3},{4,12},{12,4},... | collective-permute-start | bytes 6291464 | tf_op jit(solution)/shard_map/ppermute | solution.py:321
  121.8 11.7 %all-to-all-start = ((f32[256,1,128]{2,1,0:T(1,128)}), f32[256,1,128]{2,1,0:T(1,128)S(1)}, u32[]{:S(2)}, u32[]{:S(2)}) async-start(f32[256,1,128]{2,1,0:T(1,128)} %get-tuple-element.43), calls=%async_computation | async-start | bytes 262144 | tf_op jit(solution)/shard_map/all_to_all | solution.py:387
  134.4 12.2 %all-to-all-done.squares = f32[256,1,128]{2,1,0:T(1,128)S(1)} async-done(((f32[256,1,128]{2,1,0:T(1,128)}), f32[256,1,128]{2,1,0:T(1,128)S(1)}, u32[]{:S(2)}, u32[]{:S(2)}) %all-to-all-start) | async-done | bytes 131104 | tf_op jit(solution)/shard_map/all_to_all | solution.py:387
  146.6 4.9 %finish.1 = bf16[512,2048]{1,0:T(8,128)(2,1)} custom-call(s32[3]{0:T(128)S(1)} %pad_add_fusion.ids, f32[256,1,128]{2,1,0:T(1,128)S(1)} %all-to-all-done.squares, f32[512,1024]{1,0:T(8,128)S(1)} %get-tuple-element.44.own, f32[512,1024]{1,0:T(8,128)} %collective-permute-done.33.other), custom_call_target="tpu_custom_call" | custom-call | tf_op jit(solution)/shard_map/finish/pallas_call | solution.py:296
  (81 shorter events, 22.7 us)
Async XLA Ops:
  21.5 8.2 %collective-permute-start.2 = (f32[64,640]{1,0:T(8,128)S(1)}, f32[64,640]{1,0:T(8,128)S(1)}, u32[]{:S(2)}, u32[]{:S(2)}) collective-permute-start(f32[64,640]{1,0:T(8,128)S(1)} %get-tuple-element.30), channel_id=1, source_target_pairs={{0,32},{32,64},{64,96},{96,128},{128,160},{160,192},{192,224},{224... | collective-permute-start | bytes 491528 | tf_op jit(solution)/shard_map/ppermute | solution.py:317
  21.6 8.2 %collective-permute-start.14 = (f32[64,640]{1,0:T(8,128)S(1)}, f32[64,640]{1,0:T(8,128)S(1)}, u32[]{:S(2)}, u32[]{:S(2)}) collective-permute-start(f32[64,640]{1,0:T(8,128)S(1)} %get-tuple-element.41), channel_id=1, source_target_pairs={{0,224},{32,0},{64,32},{96,64},{128,96},{160,128},{192,160},{224,1... | collective-permute-start | bytes 491528 | tf_op jit(solution)/shard_map/ppermute | solution.py:317
  25.5 7.1 %collective-permute-start.6 = (f32[64,640]{1,0:T(8,128)S(1)}, f32[64,640]{1,0:T(8,128)S(1)}, u32[]{:S(2)}, u32[]{:S(2)}) collective-permute-start(f32[64,640]{1,0:T(8,128)S(1)} %get-tuple-element.33), channel_id=1, source_target_pairs={{0,224},{32,0},{64,32},{96,64},{128,96},{160,128},{192,160},{224,1... | collective-permute-start | bytes 491528 | tf_op jit(solution)/shard_map/ppermute | solution.py:317
  26.8 9.8 %collective-permute-start.11 = (f32[64,640]{1,0:T(8,128)S(1)}, f32[64,640]{1,0:T(8,128)S(1)}, u32[]{:S(2)}, u32[]{:S(2)}) collective-permute-start(f32[64,640]{1,0:T(8,128)S(1)} %get-tuple-element.37), channel_id=1, source_target_pairs={{0,32},{32,64},{64,96},{96,128},{128,160},{160,192},{192,224},{224... | collective-permute-start | bytes 491528 | tf_op jit(solution)/shard_map/ppermute | solution.py:317
  29.7 7.3 %collective-permute-start.3 = (f32[64,640]{1,0:T(8,128)S(1)}, f32[64,640]{1,0:T(8,128)S(1)}, u32[]{:S(2)}, u32[]{:S(2)}) collective-permute-start(f32[64,640]{1,0:T(8,128)S(1)} %add.69), channel_id=1, source_target_pairs={{0,32},{32,64},{64,96},{96,128},{128,160},{160,192},{192,224},{224... | collective-permute-start | bytes 491528 | tf_op jit(solution)/shard_map/ppermute | solution.py:317
  29.8 7.3 %collective-permute-start.15 = (f32[64,640]{1,0:T(8,128)S(1)}, f32[64,640]{1,0:T(8,128)S(1)}, u32[]{:S(2)}, u32[]{:S(2)}) collective-permute-start(f32[64,640]{1,0:T(8,128)S(1)} %add.84), channel_id=1, source_target_pairs={{0,224},{32,0},{64,32},{96,64},{128,96},{160,128},{192,160},{224,1... | collective-permute-start | bytes 491528 | tf_op jit(solution)/shard_map/ppermute | solution.py:317
  33.5 8.5 %collective-permute-start.7 = (f32[64,640]{1,0:T(8,128)S(1)}, f32[64,640]{1,0:T(8,128)S(1)}, u32[]{:S(2)}, u32[]{:S(2)}) collective-permute-start(f32[64,640]{1,0:T(8,128)S(1)} %add.73), channel_id=1, source_target_pairs={{0,224},{32,0},{64,32},{96,64},{128,96},{160,128},{192,160},{224,1... | collective-permute-start | bytes 491528 | tf_op jit(solution)/shard_map/ppermute | solution.py:317
  36.7 7.2 %collective-permute-start.12 = (f32[64,640]{1,0:T(8,128)S(1)}, f32[64,640]{1,0:T(8,128)S(1)}, u32[]{:S(2)}, u32[]{:S(2)}) collective-permute-start(f32[64,640]{1,0:T(8,128)S(1)} %add.81), channel_id=1, source_target_pairs={{0,32},{32,64},{64,96},{96,128},{128,160},{160,192},{192,224},{224... | collective-permute-start | bytes 491528 | tf_op jit(solution)/shard_map/ppermute | solution.py:317
  37.0 8.6 %collective-permute-start.4 = (f32[64,640]{1,0:T(8,128)S(1)}, f32[64,640]{1,0:T(8,128)S(1)}, u32[]{:S(2)}, u32[]{:S(2)}) collective-permute-start(f32[64,640]{1,0:T(8,128)S(1)} %add.70), channel_id=1, source_target_pairs={{0,32},{32,64},{64,96},{96,128},{128,160},{160,192},{192,224},{224... | collective-permute-start | bytes 491528 | tf_op jit(solution)/shard_map/ppermute | solution.py:317
  37.2 8.6 %collective-permute-start.16 = (f32[64,640]{1,0:T(8,128)S(1)}, f32[64,640]{1,0:T(8,128)S(1)}, u32[]{:S(2)}, u32[]{:S(2)}) collective-permute-start(f32[64,640]{1,0:T(8,128)S(1)} %add.85), channel_id=1, source_target_pairs={{0,224},{32,0},{64,32},{96,64},{128,96},{160,128},{192,160},{224,1... | collective-permute-start | bytes 491528 | tf_op jit(solution)/shard_map/ppermute | solution.py:317
  40.1 8.5 %collective-permute-start.9 = (f32[32,1024]{1,0:T(8,128)S(1)}, f32[32,1024]{1,0:T(8,128)S(1)}, u32[]{:S(2)}, u32[]{:S(2)}) collective-permute-start(f32[32,1024]{1,0:T(8,128)S(1)} %get-tuple-element.58), channel_id=1, source_target_pairs={{0,8},{8,0},{1,9},{9,1},{2,10},{10,2},{3,11},{11,3},{4,12},{12,4},... | collective-permute-start | bytes 393224 | tf_op jit(solution)/shard_map/ppermute | solution.py:321
  42.0 6.6 %collective-permute-start.8 = (f32[64,640]{1,0:T(8,128)S(1)}, f32[64,640]{1,0:T(8,128)S(1)}, u32[]{:S(2)}, u32[]{:S(2)}) collective-permute-start(f32[64,640]{1,0:T(8,128)S(1)} %add.74), channel_id=1, source_target_pairs={{0,224},{32,0},{64,32},{96,64},{128,96},{160,128},{192,160},{224,1... | collective-permute-start | bytes 491528 | tf_op jit(solution)/shard_map/ppermute | solution.py:317
  45.7 6.4 %collective-permute-start.5 = (f32[64,640]{1,0:T(8,128)S(1)}, f32[64,640]{1,0:T(8,128)S(1)}, u32[]{:S(2)}, u32[]{:S(2)}) collective-permute-start(f32[64,640]{1,0:T(8,128)S(1)} %add.71), channel_id=1, source_target_pairs={{0,32},{32,64},{64,96},{96,128},{128,160},{160,192},{192,224},{224... | collective-permute-start | bytes 491528 | tf_op jit(solution)/shard_map/ppermute | solution.py:317
  62.0 6.9 %collective-permute-start.22 = (f32[64,640]{1,0:T(8,128)S(1)}, f32[64,640]{1,0:T(8,128)S(1)}, u32[]{:S(2)}, u32[]{:S(2)}) collective-permute-start(f32[64,640]{1,0:T(8,128)S(1)} %collective-permute-done.20.refs_3_), channel_id=1, source_target_pairs={{0,224},{32,0},{64,32},{96,64},{128,96},{160,128},{192,160},{224,1... | collective-permute-start | bytes 491528 | tf_op jit(solution)/shard_map/ppermute | solution.py:317
  63.9 7.3 %collective-permute-start.26 = (f32[64,640]{1,0:T(8,128)S(1)}, f32[64,640]{1,0:T(8,128)S(1)}, u32[]{:S(2)}, u32[]{:S(2)}) collective-permute-start(f32[64,640]{1,0:T(8,128)S(1)} %collective-permute-done.25.refs_14_), channel_id=1, source_target_pairs={{0,32},{32,64},{64,96},{96,128},{128,160},{160,192},{192,224},{224... | collective-permute-start | bytes 491528 | tf_op jit(solution)/shard_map/ppermute | solution.py:317
  65.6 8.8 %collective-permute-start.31 = (f32[64,640]{1,0:T(8,128)S(1)}, f32[64,640]{1,0:T(8,128)S(1)}, u32[]{:S(2)}, u32[]{:S(2)}) collective-permute-start(f32[64,640]{1,0:T(8,128)S(1)} %collective-permute-done.30.refs_15_), channel_id=1, source_target_pairs={{0,32},{32,64},{64,96},{96,128},{128,160},{160,192},{192,224},{224... | collective-permute-start | bytes 491528 | tf_op jit(solution)/shard_map/ppermute | solution.py:317
  66.8 7.7 %collective-permute-start.21 = (f32[64,640]{1,0:T(8,128)S(1)}, f32[64,640]{1,0:T(8,128)S(1)}, u32[]{:S(2)}, u32[]{:S(2)}) collective-permute-start(f32[64,640]{1,0:T(8,128)S(1)} %collective-permute-done.19.refs_2_), channel_id=1, source_target_pairs={{0,224},{32,0},{64,32},{96,64},{128,96},{160,128},{192,160},{224,1... | collective-permute-start | bytes 491528 | tf_op jit(solution)/shard_map/ppermute | solution.py:317
  68.9 8.2 %collective-permute-start.24 = (f32[64,640]{1,0:T(8,128)S(1)}, f32[64,640]{1,0:T(8,128)S(1)}, u32[]{:S(2)}, u32[]{:S(2)}) collective-permute-start(f32[64,640]{1,0:T(8,128)S(1)} %collective-permute-done.22.refs_5_), channel_id=1, source_target_pairs={{0,224},{32,0},{64,32},{96,64},{128,96},{160,128},{192,160},{224,1... | collective-permute-start | bytes 491528 | tf_op jit(solution)/shard_map/ppermute | solution.py:317
  71.1 6.5 %collective-permute-start.27 = (f32[64,640]{1,0:T(8,128)S(1)}, f32[64,640]{1,0:T(8,128)S(1)}, u32[]{:S(2)}, u32[]{:S(2)}) collective-permute-start(f32[64,640]{1,0:T(8,128)S(1)} %collective-permute-done.26.refs_12_), channel_id=1, source_target_pairs={{0,32},{32,64},{64,96},{96,128},{128,160},{160,192},{192,224},{224... | collective-permute-start | bytes 491528 | tf_op jit(solution)/shard_map/ppermute | solution.py:317
  74.5 6.6 %collective-permute-start.32 = (f32[64,640]{1,0:T(8,128)S(1)}, f32[64,640]{1,0:T(8,128)S(1)}, u32[]{:S(2)}, u32[]{:S(2)}) collective-permute-start(f32[64,640]{1,0:T(8,128)S(1)} %collective-permute-done.31.refs_13_), channel_id=1, source_target_pairs={{0,32},{32,64},{64,96},{96,128},{128,160},{160,192},{192,224},{224... | collective-permute-start | bytes 491528 | tf_op jit(solution)/shard_map/ppermute | solution.py:317
  74.5 6.6 %collective-permute-start.23 = (f32[64,640]{1,0:T(8,128)S(1)}, f32[64,640]{1,0:T(8,128)S(1)}, u32[]{:S(2)}, u32[]{:S(2)}) collective-permute-start(f32[64,640]{1,0:T(8,128)S(1)} %collective-permute-done.21.refs_4_), channel_id=1, source_target_pairs={{0,224},{32,0},{64,32},{96,64},{128,96},{160,128},{192,160},{224,1... | collective-permute-start | bytes 491528 | tf_op jit(solution)/shard_map/ppermute | solution.py:317
  110.2 36.3 %collective-permute-start.33 = (f32[512,1024]{1,0:T(8,128)}, f32[512,1024]{1,0:T(8,128)}, u32[]{:S(2)}, u32[]{:S(2)}) collective-permute-start(f32[512,1024]{1,0:T(8,128)} %get-tuple-element.45), channel_id=1, source_target_pairs={{0,8},{8,0},{1,9},{9,1},{2,10},{10,2},{3,11},{11,3},{4,12},{12,4},... | collective-permute-start | bytes 6291464 | tf_op jit(solution)/shard_map/ppermute | solution.py:321
  121.7 11.8 %collective-permute-start.34 = (f32[64,1024]{1,0:T(8,128)S(1)}, f32[64,1024]{1,0:T(8,128)S(1)}, u32[]{:S(2)}, u32[]{:S(2)}) collective-permute-start(f32[64,1024]{1,0:T(8,128)S(1)} %get-tuple-element.54), channel_id=1, source_target_pairs={{0,8},{8,0},{1,9},{9,1},{2,10},{10,2},{3,11},{11,3},{4,12},{12,4},... | collective-permute-start | bytes 786440 | tf_op jit(solution)/shard_map/ppermute | solution.py:321
  121.8 24.8 %all-to-all-start = ((f32[256,1,128]{2,1,0:T(1,128)}), f32[256,1,128]{2,1,0:T(1,128)S(1)}, u32[]{:S(2)}, u32[]{:S(2)}) async-start(f32[256,1,128]{2,1,0:T(1,128)} %get-tuple-element.43), calls=%async_computation | async-start | bytes 262144 | tf_op jit(solution)/shard_map/all_to_all | solution.py:387
  (17 other events, 138.8 us)

commit v2 on v1

--- a/solution.py
+++ b/solution.py
@@ -29,14 +29,6 @@
         return carry
 
     lax.fori_loop(0, count, turn, 0)
-
-
-def for_halves(body, half):
-    def turn(i, carry):
-        body(pl.ds(pl.multiple_of(i * half, half), half), i)
-        return carry
-
-    lax.fori_loop(0, 2, turn, 0)
 
 
 def held(shape, index=None):
@@ -70,7 +62,7 @@
 
 
 def whiten_kernel(ids, acts, g_own, g_other, r_own, r_other, wide, gsq, *rest):
-    pieces, (block, g, r, grad, tile_sems, sems) = rest[:-6], rest[-6:]
+    pieces, (block, g, turned, r, grad, tile_sems, sems) = rest[:-7], rest[-7:]
     core = ids[0]
     half = g_own.shape[1]
     size = block.shape[1]
@@ -96,11 +88,12 @@
     for i, who in enumerate((core, 1 - core)):
         first = pl.multiple_of(who * half, half)
         copies[i].wait()
+        turned[...] = g[i].T
 
         def fill_grad(cols, j):
             if i == 0:
                 tile_copy(j).wait()
-            t = tdot(g[i], block[:, cols]).astype(bf16)
+            t = dot(turned[...], block[:, cols]).astype(bf16)
             grad[pl.ds(first, half), cols] = t
             gsq[0, 0] += jnp.sum(jnp.square(t.astype(f32)))
 
@@ -113,15 +106,17 @@
             wide[pl.ds(first, half), cols] = dot(r[i], grad[:, cols]).astype(bf16)
 
         tiles(size // TILE, fill_white)
-    wide[:, size:] = wide[:, : (DISTANCES - 1) * SLAB]
-    for k in range(size // SLAB):
+    wide[:, size:] = wide[:, : DISTANCES * SLAB]
+    span = DISTANCES * SLAB
+    for k in range(0, size // SLAB, 2):
         first = pl.multiple_of(slab(ids, k) * SLAB, SLAB)
-        t = tdot(wide[:, pl.ds(first, SLAB)], wide[:, pl.ds(first, DISTANCES * SLAB)])
-        pieces[2 * k][...] = t[:cut]
-        pieces[2 * k + 1][...] = t[cut:]
-
-
-WHITEN_MIB = 52
+        t = tdot(wide[:, pl.ds(first, 2 * SLAB)], wide[:, pl.ds(first, span + SLAB)])
+        for i in range(4):
+            left = i // 2 * SLAB
+            pieces[2 * k + i][...] = t[i * cut : (i + 1) * cut, left : left + span]
+
+
+WHITEN_MIB = 51
 PIECE = (SLAB // 2, DISTANCES * SLAB)
 
 
@@ -129,7 +124,7 @@
     tok, half = g_own.shape
     size = r_own.shape[1]
     count = 2 * size // SLAB
-    wide = (size, size + (DISTANCES - 1) * SLAB)
+    wide = (size, size + DISTANCES * SLAB)
     return call(
         whiten_kernel,
         [(wide, bf16), ((1, 1), f32)] + [(PIECE, f32)] * count,
@@ -138,6 +133,7 @@
         [
             pltpu.VMEM((tok, size), bf16),
             pltpu.VMEM((2, tok, half), bf16),
+            pltpu.VMEM((half, tok), bf16),
             pltpu.VMEM((2, half, size), bf16),
             pltpu.VMEM((size, size), bf16),
             pltpu.SemaphoreType.DMA((size // TILE,)),
@@ -211,31 +207,21 @@
     half = size // 2
 
     def fill_z(cols, j):
-        for_halves(lambda rows, i: fill_z_half(rows, cols, i, j), half)
-
-    def fill_z_half(rows, cols, i, j):
-        eye = eye_tile((half, TILE), i * half, j * TILE)
-        v = dot(yh[rows, :], yh[:, cols]) + (
-            dot(yh[rows, :], yl[:, cols]) + dot(yl[rows, :], yh[:, cols])
-        )
-        zh[rows, cols], zl[rows, cols] = halves(v)
-        q = jnp.where(eye, 1.6875, 0.0) - 0.5625 * y[rows, cols] + 0.0625 * v
-        qh[rows, cols], ql[rows, cols] = halves(q)
+        eye = eye_tile((size, TILE), 0, j * TILE)
+        v = dot(yh[...], yh[:, cols]) + (dot(yh[...], yl[:, cols]) + dot(yl[...], yh[:, cols]))
+        zh[:, cols], zl[:, cols] = halves(v)
+        q = jnp.where(eye, 1.6875, 0.0) - 0.5625 * y[:, cols] + 0.0625 * v
+        qh[:, cols], ql[:, cols] = halves(q)
 
     tiles(size // TILE, fill_z)
     scale = lax.rsqrt(jnp.full((1, 1), norm, f32))
 
     def fill_root(cols, j):
-        for_halves(lambda rows, i: fill_root_half(rows, cols, i, j), half)
-
-    def fill_root_half(rows, cols, i, j):
-        eye = eye_tile((half, TILE), i * half, j * TILE)
-        v = dot(zh[rows, :], qh[:, cols]) + (
-            dot(zh[rows, :], ql[:, cols]) + dot(zl[rows, :], qh[:, cols])
-        )
-        v = (jnp.where(eye, 2.25, 0.0) - 2.4375 * y[rows, cols] + v) * scale
-        root[rows, cols] = v
-        rh[rows, cols] = v.astype(bf16)
+        eye = eye_tile((size, TILE), 0, j * TILE)
+        v = dot(zh[...], qh[:, cols]) + (dot(zh[...], ql[:, cols]) + dot(zl[...], qh[:, cols]))
+        v = (jnp.where(eye, 2.25, 0.0) - 2.4375 * y[:, cols] + v) * scale
+        root[:, cols] = v
+        rh[:, cols] = v.astype(bf16)
 
     tiles(size // TILE, fill_root)
     keep(root, 1)

time: 152 us -> 151 us (level)
  waiting for transfers between devices: 39.4 us -> 35.7 us
  starting transfers between devices: 64.4 us -> 68 us
    ppermute x28, starting transfers between devices: 34.3 us -> 39.4 us  [shift(): return lax.ppermute(x, 'z', [(i, (i + by) % count) for i in range(count)])]
    ppermute x7, starting transfers between devices: 18.4 us -> 14.1 us  [swap(): return lax.ppermute(x, axis, [(0, 1), (1, 0)])]
    all_to_all x1, starting transfers between devices: 11.7 us -> 14.5 us  [shards(): squares = lax.all_to_all(squares, peers, 0, 0, tiled=True)]
    ppermute x28, waiting for transfers between devices: 20.6 us -> 17.9 us  [shift(): return lax.ppermute(x, 'z', [(i, (i + by) % count) for i in range(count)])]
    pallas_call x1, Pallas kernels: 26.2 us -> 24.7 us  [root(): call(root_kernel, [((size // 2, size), f32)] * 2 + [((rows, size), f32),...]
where the time goes in v2:
time: 151 us
  starting transfers between devices  68 us (45%)
  Pallas kernels  43.8 us (29%)
  waiting for transfers between devices  35.7 us (24%)
  local copies, waits for them, and re-layouts  1.87 us (1%)
    ppermute x28, starting transfers between devices, shift(): return lax.ppermute(x, 'z', [(i, (i + by) % count) for i in range(count)])  39.4 us
    pallas_call x1, Pallas kernels, root(): call(root_kernel, [((size // 2, size), f32)] * 2 + [((rows, size), f32),...  24.7 us
    ppermute x28, waiting for transfers between devices, shift(): return lax.ppermute(x, 'z', [(i, (i + by) % count) for i in range(count)])  17.9 us
    all_to_all x1, starting transfers between devices, shards(): squares = lax.all_to_all(squares, peers, 0, 0, tiled=True)  14.5 us
    pallas_call x1, Pallas kernels, whiten(): call(whiten_kernel, [(wide, bf16), ((1, 1), f32)] + [(PIECE, f32)] * coun...  14.2 us
    ppermute x7, starting transfers between devices, swap(): return lax.ppermute(x, axis, [(0, 1), (1, 0)])  14.1 us
    all_to_all x1, waiting for transfers between devices, shards(): squares = lax.all_to_all(squares, peers, 0, 0, tiled=True)  12.2 us
    ppermute x7, waiting for transfers between devices, swap(): return lax.ppermute(x, axis, [(0, 1), (1, 0)])  5.69 us
  transfers between devices with their start and end apart: 36, of which 17 were waited for; matrix products, arithmetic and copies ran while one was open for 1% of the time, Pallas kernels for 0%

profile of v2, /device:TPU:1, one launch (start us, length us, event | category | flops | bytes accessed | tf_op | source)
XLA Modules:
  0.0 150.7 jit_solution(11369414612108340632)
XLA Ops:
  0.6 3.3 %collective-permute-start = (bf16[1024,512]{1,0:T(8,128)(2,1)}, bf16[1024,512]{1,0:T(8,128)(2,1)S(1)}, u32[]{:S(2)}, u32[]{:S(2)}) collective-permute-start(bf16[1024,512]{1,0:T(8,128)(2,1)} %g_own.1), channel_id=1, source_target_pairs={{0,8},{8,0},{1,9},{9,1},{2,10},{10,2},{3,11},{11,3},{4,12},{12,4},... | collective-permute-start | bytes 3145736 | tf_op jit(solution)/shard_map/ppermute | solution.py:307
  4.1 2.8 %collective-permute-done.g_other = bf16[1024,512]{1,0:T(8,128)(2,1)S(1)} collective-permute-done((bf16[1024,512]{1,0:T(8,128)(2,1)}, bf16[1024,512]{1,0:T(8,128)(2,1)S(1)}, u32[]{:S(2)}, u32[]{:S(2)}) %collective-permute-start) | collective-permute-done | bytes 1048608 | tf_op jit(solution)/shard_map/ppermute | solution.py:307
  8.1 14.2 %whiten.1 = (bf16[1024,1664]{1,0:T(8,128)(2,1)}, f32[1,1]{1,0:T(1,128)}, f32[64,640]{1,0:T(8,128)S(1)}, f32[64,640]{1,0:T(8,128)S(1)}, f32[64,640]{1,0:T(8,128)S...) custom-call(s32[3]{0:T(128)S(1)} %pad_add_fusion.ids, ...), custom_call_target="tpu_custom_call" | custom-call | flops 5637144576 | bytes 8388608 | tf_op jit(solution)/shard_map/whiten/pallas_call | solution.py:128
  22.4 3.9 %collective-permute-start.14 = (f32[64,640]{1,0:T(8,128)S(1)}, f32[64,640]{1,0:T(8,128)S(1)}, u32[]{:S(2)}, u32[]{:S(2)}) collective-permute-start(f32[64,640]{1,0:T(8,128)S(1)} %get-tuple-element.41), channel_id=1, source_target_pairs={{0,224},{32,0},{64,32},{96,64},{128,96},{160,128},{192,160},{224,1... | collective-permute-start | bytes 491528 | tf_op jit(solution)/shard_map/ppermute | solution.py:303
  27.8 2.7 %collective-permute-done.2 = f32[64,640]{1,0:T(8,128)S(1)} collective-permute-done((f32[64,640]{1,0:T(8,128)S(1)}, f32[64,640]{1,0:T(8,128)S(1)}, u32[]{:S(2)}, u32[]{:S(2)}) %collective-permute-start.2) | collective-permute-done | bytes 163872 | tf_op jit(solution)/shard_map/ppermute | solution.py:303
  30.6 2.7 %collective-permute-start.15 = (f32[64,640]{1,0:T(8,128)S(1)}, f32[64,640]{1,0:T(8,128)S(1)}, u32[]{:S(2)}, u32[]{:S(2)}) collective-permute-start(f32[64,640]{1,0:T(8,128)S(1)} %add.84), channel_id=1, source_target_pairs={{0,224},{32,0},{64,32},{96,64},{128,96},{160,128},{192,160},{224,1... | collective-permute-start | bytes 491528 | tf_op jit(solution)/shard_map/ppermute | solution.py:303
  33.4 3.1 %collective-permute-start.7 = (f32[64,640]{1,0:T(8,128)S(1)}, f32[64,640]{1,0:T(8,128)S(1)}, u32[]{:S(2)}, u32[]{:S(2)}) collective-permute-start(f32[64,640]{1,0:T(8,128)S(1)} %add.73), channel_id=1, source_target_pairs={{0,224},{32,0},{64,32},{96,64},{128,96},{160,128},{192,160},{224,1... | collective-permute-start | bytes 491528 | tf_op jit(solution)/shard_map/ppermute | solution.py:303
  38.0 2.9 %collective-permute-start.16 = (f32[64,640]{1,0:T(8,128)S(1)}, f32[64,640]{1,0:T(8,128)S(1)}, u32[]{:S(2)}, u32[]{:S(2)}) collective-permute-start(f32[64,640]{1,0:T(8,128)S(1)} %add.85), channel_id=1, source_target_pairs={{0,224},{32,0},{64,32},{96,64},{128,96},{160,128},{192,160},{224,1... | collective-permute-start | bytes 491528 | tf_op jit(solution)/shard_map/ppermute | solution.py:303
  40.9 2.0 %collective-permute-start.9 = (f32[32,1024]{1,0:T(8,128)S(1)}, f32[32,1024]{1,0:T(8,128)S(1)}, u32[]{:S(2)}, u32[]{:S(2)}) collective-permute-start(f32[32,1024]{1,0:T(8,128)S(1)} %get-tuple-element.58), channel_id=1, source_target_pairs={{0,8},{8,0},{1,9},{9,1},{2,10},{10,2},{3,11},{11,3},{4,12},{12,4},... | collective-permute-start | bytes 393224 | tf_op jit(solution)/shard_map/ppermute | solution.py:307
  45.7 2.7 %collective-permute-start.17 = (f32[64,640]{1,0:T(8,128)S(1)}, f32[64,640]{1,0:T(8,128)S(1)}, u32[]{:S(2)}, u32[]{:S(2)}) collective-permute-start(f32[64,640]{1,0:T(8,128)S(1)} %add.86), channel_id=1, source_target_pairs={{0,224},{32,0},{64,32},{96,64},{128,96},{160,128},{192,160},{224,1... | collective-permute-start | bytes 491528 | tf_op jit(solution)/shard_map/ppermute | solution.py:303
  49.2 2.7 %collective-permute-done.5 = f32[64,640]{1,0:T(8,128)S(1)} collective-permute-done((f32[64,640]{1,0:T(8,128)S(1)}, f32[64,640]{1,0:T(8,128)S(1)}, u32[]{:S(2)}, u32[]{:S(2)}) %collective-permute-start.5) | collective-permute-done | bytes 163872 | tf_op jit(solution)/shard_map/ppermute | solution.py:303
  53.6 2.7 %collective-permute-done.18 = f32[64,640]{1,0:T(8,128)S(1)} collective-permute-done((f32[64,640]{1,0:T(8,128)S(1)}, f32[64,640]{1,0:T(8,128)S(1)}, u32[]{:S(2)}, u32[]{:S(2)}) %collective-permute-start.18) | collective-permute-done | bytes 163872 | tf_op jit(solution)/shard_map/ppermute | solution.py:307
  56.3 1.9 %collective-permute-start.20 = (f32[64,640]{1,0:T(8,128)S(1)}, f32[64,640]{1,0:T(8,128)S(1)}, u32[]{:S(2)}, u32[]{:S(2)}) collective-permute-start(f32[64,640]{1,0:T(8,128)S(1)} %add.89.refs_1_), channel_id=1, source_target_pairs={{0,224},{32,0},{64,32},{96,64},{128,96},{160,128},{192,160},{224,1... | collective-permute-start | bytes 491528 | tf_op jit(solution)/shard_map/ppermute | solution.py:303
  60.4 1.9 %collective-permute-start.19 = (f32[64,640]{1,0:T(8,128)S(1)}, f32[64,640]{1,0:T(8,128)S(1)}, u32[]{:S(2)}, u32[]{:S(2)}) collective-permute-start(f32[64,640]{1,0:T(8,128)S(1)} %add.80.refs_0_), channel_id=1, source_target_pairs={{0,224},{32,0},{64,32},{96,64},{128,96},{160,128},{192,160},{224,1... | collective-permute-start | bytes 491528 | tf_op jit(solution)/shard_map/ppermute | solution.py:303
  62.3 3.4 %collective-permute-start.22 = (f32[64,640]{1,0:T(8,128)S(1)}, f32[64,640]{1,0:T(8,128)S(1)}, u32[]{:S(2)}, u32[]{:S(2)}) collective-permute-start(f32[64,640]{1,0:T(8,128)S(1)} %collective-permute-done.20.refs_3_), channel_id=1, source_target_pairs={{0,224},{32,0},{64,32},{96,64},{128,96},{160,128},{192,160},{224,1... | collective-permute-start | bytes 491528 | tf_op jit(solution)/shard_map/ppermute | solution.py:303
  67.3 4.6 %collective-permute-start.21 = (f32[64,640]{1,0:T(8,128)S(1)}, f32[64,640]{1,0:T(8,128)S(1)}, u32[]{:S(2)}, u32[]{:S(2)}) collective-permute-start(f32[64,640]{1,0:T(8,128)S(1)} %collective-permute-done.19.refs_2_), channel_id=1, source_target_pairs={{0,224},{32,0},{64,32},{96,64},{128,96},{160,128},{192,160},{224,1... | collective-permute-start | bytes 491528 | tf_op jit(solution)/shard_map/ppermute | solution.py:303
  75.2 3.6 %collective-permute-start.23 = (f32[64,640]{1,0:T(8,128)S(1)}, f32[64,640]{1,0:T(8,128)S(1)}, u32[]{:S(2)}, u32[]{:S(2)}) collective-permute-start(f32[64,640]{1,0:T(8,128)S(1)} %collective-permute-done.21.refs_4_), channel_id=1, source_target_pairs={{0,224},{32,0},{64,32},{96,64},{128,96},{160,128},{192,160},{224,1... | collective-permute-start | bytes 491528 | tf_op jit(solution)/shard_map/ppermute | solution.py:303
  80.3 2.0 %collective-permute-done.32.refs_11_ = f32[64,640]{1,0:T(8,128)S(1)} collective-permute-done((f32[64,640]{1,0:T(8,128)S(1)}, f32[64,640]{1,0:T(8,128)S(1)}, u32[]{:S(2)}, u32[]{:S(2)}) %collective-permute-start.32) | collective-permute-done | bytes 163872 | tf_op jit(solution)/shard_map/ppermute | solution.py:303
  84.6 1.9 %collective-permute-done.28.refs_8_ = f32[64,640]{1,0:T(8,128)S(1)} collective-permute-done((f32[64,640]{1,0:T(8,128)S(1)}, f32[64,640]{1,0:T(8,128)S(1)}, u32[]{:S(2)}, u32[]{:S(2)}) %collective-permute-start.28) | collective-permute-done | bytes 163872 | tf_op jit(solution)/shard_map/ppermute | solution.py:303
  86.4 24.7 %root.1 = (f32[512,1024]{1,0:T(8,128)S(1)}, f32[512,1024]{1,0:T(8,128)}, f32[128,1024]{1,0:T(8,128)S(1)}, f32[256,1,128]{2,1,0:T(1,128)}) custom-call(s32[3]{0:T(128)S(1)} %pad_add_fusion.ids, f32[1,1]{1,0:T(1,128)} %get-tuple-element.25.gsq, f32[64,640]{1,0:T(8,128)S(1)} %add.80.refs_0_, f32[64,640]{1,0:T(8,128)S(1)} %add.89.refs_1_, ...), custom_call_target="tpu_custom_call" | custom-call | flops 15032385536 | bytes 8388608 | tf_op jit(solution)/shard_map/root/pallas_call | solution.py:250
  111.1 7.0 %collective-permute-start.33 = (f32[512,1024]{1,0:T(8,128)}, f32[512,1024]{1,0:T(8,128)}, u32[]{:S(2)}, u32[]{:S(2)}) collective-permute-start(f32[512,1024]{1,0:T(8,128)} %get-tuple-element.45), channel_id=1, source_target_pairs={{0,8},{8,0},{1,9},{9,1},{2,10},{10,2},{3,11},{11,3},{4,12},{12,4},... | collective-permute-start | bytes 6291464 | tf_op jit(solution)/shard_map/ppermute | solution.py:307
  118.3 14.5 %all-to-all-start = ((f32[256,1,128]{2,1,0:T(1,128)}), f32[256,1,128]{2,1,0:T(1,128)S(1)}, u32[]{:S(2)}, u32[]{:S(2)}) async-start(f32[256,1,128]{2,1,0:T(1,128)} %get-tuple-element.43), calls=%async_computation | async-start | bytes 262144 | tf_op jit(solution)/shard_map/all_to_all | solution.py:373
  133.7 12.2 %all-to-all-done.squares = f32[256,1,128]{2,1,0:T(1,128)S(1)} async-done(((f32[256,1,128]{2,1,0:T(1,128)}), f32[256,1,128]{2,1,0:T(1,128)S(1)}, u32[]{:S(2)}, u32[]{:S(2)}) %all-to-all-start) | async-done | bytes 131104 | tf_op jit(solution)/shard_map/all_to_all | solution.py:373
  145.8 4.9 %finish.1 = bf16[512,2048]{1,0:T(8,128)(2,1)} custom-call(s32[3]{0:T(128)S(1)} %pad_add_fusion.ids, f32[256,1,128]{2,1,0:T(1,128)S(1)} %all-to-all-done.squares, f32[512,1024]{1,0:T(8,128)S(1)} %get-tuple-element.44.own, f32[512,1024]{1,0:T(8,128)} %collective-permute-done.33.other), custom_call_target="tpu_custom_call" | custom-call | tf_op jit(solution)/shard_map/finish/pallas_call | solution.py:282
  (75 shorter events, 21.5 us)
Async XLA Ops:
  22.3 8.2 %collective-permute-start.2 = (f32[64,640]{1,0:T(8,128)S(1)}, f32[64,640]{1,0:T(8,128)S(1)}, u32[]{:S(2)}, u32[]{:S(2)}) collective-permute-start(f32[64,640]{1,0:T(8,128)S(1)} %get-tuple-element.30), channel_id=1, source_target_pairs={{0,32},{32,64},{64,96},{96,128},{128,160},{160,192},{192,224},{224... | collective-permute-start | bytes 491528 | tf_op jit(solution)/shard_map/ppermute | solution.py:303
  22.4 8.2 %collective-permute-start.14 = (f32[64,640]{1,0:T(8,128)S(1)}, f32[64,640]{1,0:T(8,128)S(1)}, u32[]{:S(2)}, u32[]{:S(2)}) collective-permute-start(f32[64,640]{1,0:T(8,128)S(1)} %get-tuple-element.41), channel_id=1, source_target_pairs={{0,224},{32,0},{64,32},{96,64},{128,96},{160,128},{192,160},{224,1... | collective-permute-start | bytes 491528 | tf_op jit(solution)/shard_map/ppermute | solution.py:303
  26.3 7.1 %collective-permute-start.6 = (f32[64,640]{1,0:T(8,128)S(1)}, f32[64,640]{1,0:T(8,128)S(1)}, u32[]{:S(2)}, u32[]{:S(2)}) collective-permute-start(f32[64,640]{1,0:T(8,128)S(1)} %get-tuple-element.33), channel_id=1, source_target_pairs={{0,224},{32,0},{64,32},{96,64},{128,96},{160,128},{192,160},{224,1... | collective-permute-start | bytes 491528 | tf_op jit(solution)/shard_map/ppermute | solution.py:303
  27.7 8.9 %collective-permute-start.11 = (f32[64,640]{1,0:T(8,128)S(1)}, f32[64,640]{1,0:T(8,128)S(1)}, u32[]{:S(2)}, u32[]{:S(2)}) collective-permute-start(f32[64,640]{1,0:T(8,128)S(1)} %get-tuple-element.37), channel_id=1, source_target_pairs={{0,32},{32,64},{64,96},{96,128},{128,160},{160,192},{192,224},{224... | collective-permute-start | bytes 491528 | tf_op jit(solution)/shard_map/ppermute | solution.py:303
  30.5 7.3 %collective-permute-start.3 = (f32[64,640]{1,0:T(8,128)S(1)}, f32[64,640]{1,0:T(8,128)S(1)}, u32[]{:S(2)}, u32[]{:S(2)}) collective-permute-start(f32[64,640]{1,0:T(8,128)S(1)} %add.69), channel_id=1, source_target_pairs={{0,32},{32,64},{64,96},{96,128},{128,160},{160,192},{192,224},{224... | collective-permute-start | bytes 491528 | tf_op jit(solution)/shard_map/ppermute | solution.py:303
  30.6 7.3 %collective-permute-start.15 = (f32[64,640]{1,0:T(8,128)S(1)}, f32[64,640]{1,0:T(8,128)S(1)}, u32[]{:S(2)}, u32[]{:S(2)}) collective-permute-start(f32[64,640]{1,0:T(8,128)S(1)} %add.84), channel_id=1, source_target_pairs={{0,224},{32,0},{64,32},{96,64},{128,96},{160,128},{192,160},{224,1... | collective-permute-start | bytes 491528 | tf_op jit(solution)/shard_map/ppermute | solution.py:303
  33.4 9.6 %collective-permute-start.7 = (f32[64,640]{1,0:T(8,128)S(1)}, f32[64,640]{1,0:T(8,128)S(1)}, u32[]{:S(2)}, u32[]{:S(2)}) collective-permute-start(f32[64,640]{1,0:T(8,128)S(1)} %add.73), channel_id=1, source_target_pairs={{0,224},{32,0},{64,32},{96,64},{128,96},{160,128},{192,160},{224,1... | collective-permute-start | bytes 491528 | tf_op jit(solution)/shard_map/ppermute | solution.py:303
  36.6 7.2 %collective-permute-start.12 = (f32[64,640]{1,0:T(8,128)S(1)}, f32[64,640]{1,0:T(8,128)S(1)}, u32[]{:S(2)}, u32[]{:S(2)}) collective-permute-start(f32[64,640]{1,0:T(8,128)S(1)} %add.81), channel_id=1, source_target_pairs={{0,32},{32,64},{64,96},{96,128},{128,160},{160,192},{192,224},{224... | collective-permute-start | bytes 491528 | tf_op jit(solution)/shard_map/ppermute | solution.py:303
  37.9 7.7 %collective-permute-start.4 = (f32[64,640]{1,0:T(8,128)S(1)}, f32[64,640]{1,0:T(8,128)S(1)}, u32[]{:S(2)}, u32[]{:S(2)}) collective-permute-start(f32[64,640]{1,0:T(8,128)S(1)} %add.70), channel_id=1, source_target_pairs={{0,32},{32,64},{64,96},{96,128},{128,160},{160,192},{192,224},{224... | collective-permute-start | bytes 491528 | tf_op jit(solution)/shard_map/ppermute | solution.py:303
  38.0 7.7 %collective-permute-start.16 = (f32[64,640]{1,0:T(8,128)S(1)}, f32[64,640]{1,0:T(8,128)S(1)}, u32[]{:S(2)}, u32[]{:S(2)}) collective-permute-start(f32[64,640]{1,0:T(8,128)S(1)} %add.85), channel_id=1, source_target_pairs={{0,224},{32,0},{64,32},{96,64},{128,96},{160,128},{192,160},{224,1... | collective-permute-start | bytes 491528 | tf_op jit(solution)/shard_map/ppermute | solution.py:303
  40.9 7.5 %collective-permute-start.9 = (f32[32,1024]{1,0:T(8,128)S(1)}, f32[32,1024]{1,0:T(8,128)S(1)}, u32[]{:S(2)}, u32[]{:S(2)}) collective-permute-start(f32[32,1024]{1,0:T(8,128)S(1)} %get-tuple-element.58), channel_id=1, source_target_pairs={{0,8},{8,0},{1,9},{9,1},{2,10},{10,2},{3,11},{11,3},{4,12},{12,4},... | collective-permute-start | bytes 393224 | tf_op jit(solution)/shard_map/ppermute | solution.py:307
  58.3 7.4 %collective-permute-start.25 = (f32[64,640]{1,0:T(8,128)S(1)}, f32[64,640]{1,0:T(8,128)S(1)}, u32[]{:S(2)}, u32[]{:S(2)}) collective-permute-start(f32[64,640]{1,0:T(8,128)S(1)} %add.80.refs_0_), channel_id=1, source_target_pairs={{0,32},{32,64},{64,96},{96,128},{128,160},{160,192},{192,224},{224... | collective-permute-start | bytes 491528 | tf_op jit(solution)/shard_map/ppermute | solution.py:303
  58.6 8.0 %collective-permute-start.30 = (f32[64,640]{1,0:T(8,128)S(1)}, f32[64,640]{1,0:T(8,128)S(1)}, u32[]{:S(2)}, u32[]{:S(2)}) collective-permute-start(f32[64,640]{1,0:T(8,128)S(1)} %add.89.refs_1_), channel_id=1, source_target_pairs={{0,32},{32,64},{64,96},{96,128},{128,160},{160,192},{192,224},{224... | collective-permute-start | bytes 491528 | tf_op jit(solution)/shard_map/ppermute | solution.py:303
  62.3 9.6 %collective-permute-start.22 = (f32[64,640]{1,0:T(8,128)S(1)}, f32[64,640]{1,0:T(8,128)S(1)}, u32[]{:S(2)}, u32[]{:S(2)}) collective-permute-start(f32[64,640]{1,0:T(8,128)S(1)} %collective-permute-done.20.refs_3_), channel_id=1, source_target_pairs={{0,224},{32,0},{64,32},{96,64},{128,96},{160,128},{192,160},{224,1... | collective-permute-start | bytes 491528 | tf_op jit(solution)/shard_map/ppermute | solution.py:303
  65.7 7.6 %collective-permute-start.26 = (f32[64,640]{1,0:T(8,128)S(1)}, f32[64,640]{1,0:T(8,128)S(1)}, u32[]{:S(2)}, u32[]{:S(2)}) collective-permute-start(f32[64,640]{1,0:T(8,128)S(1)} %collective-permute-done.25.refs_14_), channel_id=1, source_target_pairs={{0,32},{32,64},{64,96},{96,128},{128,160},{160,192},{192,224},{224... | collective-permute-start | bytes 491528 | tf_op jit(solution)/shard_map/ppermute | solution.py:303
  66.6 8.6 %collective-permute-start.31 = (f32[64,640]{1,0:T(8,128)S(1)}, f32[64,640]{1,0:T(8,128)S(1)}, u32[]{:S(2)}, u32[]{:S(2)}) collective-permute-start(f32[64,640]{1,0:T(8,128)S(1)} %collective-permute-done.30.refs_15_), channel_id=1, source_target_pairs={{0,32},{32,64},{64,96},{96,128},{128,160},{160,192},{192,224},{224... | collective-permute-start | bytes 491528 | tf_op jit(solution)/shard_map/ppermute | solution.py:303
  67.3 7.9 %collective-permute-start.21 = (f32[64,640]{1,0:T(8,128)S(1)}, f32[64,640]{1,0:T(8,128)S(1)}, u32[]{:S(2)}, u32[]{:S(2)}) collective-permute-start(f32[64,640]{1,0:T(8,128)S(1)} %collective-permute-done.19.refs_2_), channel_id=1, source_target_pairs={{0,224},{32,0},{64,32},{96,64},{128,96},{160,128},{192,160},{224,1... | collective-permute-start | bytes 491528 | tf_op jit(solution)/shard_map/ppermute | solution.py:303
  71.9 6.9 %collective-permute-start.24 = (f32[64,640]{1,0:T(8,128)S(1)}, f32[64,640]{1,0:T(8,128)S(1)}, u32[]{:S(2)}, u32[]{:S(2)}) collective-permute-start(f32[64,640]{1,0:T(8,128)S(1)} %collective-permute-done.22.refs_5_), channel_id=1, source_target_pairs={{0,224},{32,0},{64,32},{96,64},{128,96},{160,128},{192,160},{224,1... | collective-permute-start | bytes 491528 | tf_op jit(solution)/shard_map/ppermute | solution.py:303
  73.4 6.9 %collective-permute-start.27 = (f32[64,640]{1,0:T(8,128)S(1)}, f32[64,640]{1,0:T(8,128)S(1)}, u32[]{:S(2)}, u32[]{:S(2)}) collective-permute-start(f32[64,640]{1,0:T(8,128)S(1)} %collective-permute-done.26.refs_12_), channel_id=1, source_target_pairs={{0,32},{32,64},{64,96},{96,128},{128,160},{160,192},{192,224},{224... | collective-permute-start | bytes 491528 | tf_op jit(solution)/shard_map/ppermute | solution.py:303
  75.2 7.1 %collective-permute-start.32 = (f32[64,640]{1,0:T(8,128)S(1)}, f32[64,640]{1,0:T(8,128)S(1)}, u32[]{:S(2)}, u32[]{:S(2)}) collective-permute-start(f32[64,640]{1,0:T(8,128)S(1)} %collective-permute-done.31.refs_13_), channel_id=1, source_target_pairs={{0,32},{32,64},{64,96},{96,128},{128,160},{160,192},{192,224},{224... | collective-permute-start | bytes 491528 | tf_op jit(solution)/shard_map/ppermute | solution.py:303
  75.2 7.7 %collective-permute-start.23 = (f32[64,640]{1,0:T(8,128)S(1)}, f32[64,640]{1,0:T(8,128)S(1)}, u32[]{:S(2)}, u32[]{:S(2)}) collective-permute-start(f32[64,640]{1,0:T(8,128)S(1)} %collective-permute-done.21.refs_4_), channel_id=1, source_target_pairs={{0,224},{32,0},{64,32},{96,64},{128,96},{160,128},{192,160},{224,1... | collective-permute-start | bytes 491528 | tf_op jit(solution)/shard_map/ppermute | solution.py:303
  111.1 34.7 %collective-permute-start.33 = (f32[512,1024]{1,0:T(8,128)}, f32[512,1024]{1,0:T(8,128)}, u32[]{:S(2)}, u32[]{:S(2)}) collective-permute-start(f32[512,1024]{1,0:T(8,128)} %get-tuple-element.45), channel_id=1, source_target_pairs={{0,8},{8,0},{1,9},{9,1},{2,10},{10,2},{3,11},{11,3},{4,12},{12,4},... | collective-permute-start | bytes 6291464 | tf_op jit(solution)/shard_map/ppermute | solution.py:307
  118.2 14.6 %collective-permute-start.34 = (f32[64,1024]{1,0:T(8,128)S(1)}, f32[64,1024]{1,0:T(8,128)S(1)}, u32[]{:S(2)}, u32[]{:S(2)}) collective-permute-start(f32[64,1024]{1,0:T(8,128)S(1)} %get-tuple-element.54), channel_id=1, source_target_pairs={{0,8},{8,0},{1,9},{9,1},{2,10},{10,2},{3,11},{11,3},{4,12},{12,4},... | collective-permute-start | bytes 786440 | tf_op jit(solution)/shard_map/ppermute | solution.py:307
  118.3 27.5 %all-to-all-start = ((f32[256,1,128]{2,1,0:T(1,128)}), f32[256,1,128]{2,1,0:T(1,128)S(1)}, u32[]{:S(2)}, u32[]{:S(2)}) async-start(f32[256,1,128]{2,1,0:T(1,128)} %get-tuple-element.43), calls=%async_computation | async-start | bytes 262144 | tf_op jit(solution)/shard_map/all_to_all | solution.py:373
  (14 other events, 87.9 us)

commit v3 on v2

--- a/solution.py
+++ b/solution.py
@@ -9,6 +9,7 @@
 damping = 0.001
 epsilon = 1e-06
 TILE = 256
+WIDE = 512
 SLAB = 128
 DISTANCES = 5
 f32 = jnp.float32
@@ -23,9 +24,9 @@
     return jnp.dot(a, b, preferred_element_type=f32)
 
 
-def tiles(count, body):
+def tiles(count, body, step=TILE):
     def turn(j, carry):
-        body(pl.ds(pl.multiple_of(j * TILE, TILE), TILE), j)
+        body(pl.ds(pl.multiple_of(j * step, step), step), j)
         return carry
 
     lax.fori_loop(0, count, turn, 0)
@@ -62,15 +63,15 @@
 
 
 def whiten_kernel(ids, acts, g_own, g_other, r_own, r_other, wide, gsq, *rest):
-    pieces, (block, g, turned, r, grad, tile_sems, sems) = rest[:-7], rest[-7:]
+    pieces, (block, g, r, grad, summed, tile_sems, sems) = rest[:-7], rest[-7:]
     core = ids[0]
     half = g_own.shape[1]
     size = block.shape[1]
     cut = SLAB // 2
 
     def tile_copy(j):
-        source = pl.ds(pl.multiple_of(core * size + j * TILE, TILE), TILE)
-        target = pl.ds(pl.multiple_of(j * TILE, TILE), TILE)
+        source = pl.ds(pl.multiple_of(core * size + j * WIDE, WIDE), WIDE)
+        target = pl.ds(pl.multiple_of(j * WIDE, WIDE), WIDE)
         return pltpu.make_async_copy(acts.at[:, source], block.at[:, target], tile_sems.at[j])
 
     copies = [
@@ -80,24 +81,24 @@
         )
     ]
     copies[0].start()
-    for j in range(size // TILE):
+    for j in range(size // WIDE):
         tile_copy(j).start()
     for copy in copies[1:]:
         copy.start()
-    gsq[0, 0] = 0.0
+    summed[...] = jnp.zeros_like(summed)
     for i, who in enumerate((core, 1 - core)):
         first = pl.multiple_of(who * half, half)
         copies[i].wait()
-        turned[...] = g[i].T
 
         def fill_grad(cols, j):
             if i == 0:
                 tile_copy(j).wait()
-            t = dot(turned[...], block[:, cols]).astype(bf16)
+            t = tdot(g[i], block[:, cols]).astype(bf16)
             grad[pl.ds(first, half), cols] = t
-            gsq[0, 0] += jnp.sum(jnp.square(t.astype(f32)))
-
-        tiles(size // TILE, fill_grad)
+            squares = jnp.square(t.astype(f32)).reshape(half // 8, 8, WIDE)
+            summed[...] += jnp.sum(squares, axis=0)
+
+        tiles(size // WIDE, fill_grad, WIDE)
     for i, who in enumerate((core, 1 - core)):
         first = pl.multiple_of(who * half, half)
         copies[2 + i].wait()
@@ -105,7 +106,8 @@
         def fill_white(cols, j):
             wide[pl.ds(first, half), cols] = dot(r[i], grad[:, cols]).astype(bf16)
 
-        tiles(size // TILE, fill_white)
+        tiles(size // WIDE, fill_white, WIDE)
+    gsq[0, 0] = jnp.sum(summed[...])
     wide[:, size:] = wide[:, : DISTANCES * SLAB]
     span = DISTANCES * SLAB
     for k in range(0, size // SLAB, 2):
@@ -133,10 +135,10 @@
         [
             pltpu.VMEM((tok, size), bf16),
             pltpu.VMEM((2, tok, half), bf16),
-            pltpu.VMEM((half, tok), bf16),
             pltpu.VMEM((2, half, size), bf16),
             pltpu.VMEM((size, size), bf16),
-            pltpu.SemaphoreType.DMA((size // TILE,)),
+            pltpu.VMEM((8, WIDE), f32),
+            pltpu.SemaphoreType.DMA((size // WIDE,)),
             pltpu.SemaphoreType.DMA((4,)),
         ],
         WHITEN_MIB,

time: 151 us -> 148 us (0.980)
  Pallas kernels: 43.8 us -> 41.3 us
    pallas_call x1, Pallas kernels: 14.2 us -> 11.7 us  [whiten(): call(whiten_kernel, [(wide, bf16), ((1, 1), f32)] + [(PIECE, f32)] * coun...]
where the time goes in v3:
time: 148 us
  starting transfers between devices  68 us (46%)
  Pallas kernels  41.3 us (28%)
  waiting for transfers between devices  35.7 us (24%)
  local copies, waits for them, and re-layouts  1.87 us (1%)
    ppermute x28, starting transfers between devices, shift(): return lax.ppermute(x, 'z', [(i, (i + by) % count) for i in range(count)])  39.6 us
    pallas_call x1, Pallas kernels, root(): call(root_kernel, [((size // 2, size), f32)] * 2 + [((rows, size), f32),...  24.7 us
    ppermute x28, waiting for transfers between devices, shift(): return lax.ppermute(x, 'z', [(i, (i + by) % count) for i in range(count)])  17.9 us
    all_to_all x1, starting transfers between devices, shards(): squares = lax.all_to_all(squares, peers, 0, 0, tiled=True)  14.5 us
    ppermute x7, starting transfers between devices, swap(): return lax.ppermute(x, axis, [(0, 1), (1, 0)])  13.8 us
    all_to_all x1, waiting for transfers between devices, shards(): squares = lax.all_to_all(squares, peers, 0, 0, tiled=True)  12.2 us
    pallas_call x1, Pallas kernels, whiten(): call(whiten_kernel, [(wide, bf16), ((1, 1), f32)] + [(PIECE, f32)] * coun...  11.7 us
    ppermute x7, waiting for transfers between devices, swap(): return lax.ppermute(x, axis, [(0, 1), (1, 0)])  5.69 us
  transfers between devices with their start and end apart: 36, of which 17 were waited for; matrix products, arithmetic and copies ran while one was open for 1% of the time, Pallas kernels for 0%

profile of v3, /device:TPU:1, one launch (start us, length us, event | category | flops | bytes accessed | tf_op | source)
XLA Modules:
  0.0 148.1 jit_solution(703898558000048499)
XLA Ops:
  0.6 3.3 %collective-permute-start = (bf16[1024,512]{1,0:T(8,128)(2,1)}, bf16[1024,512]{1,0:T(8,128)(2,1)S(1)}, u32[]{:S(2)}, u32[]{:S(2)}) collective-permute-start(bf16[1024,512]{1,0:T(8,128)(2,1)} %g_own.1), channel_id=1, source_target_pairs={{0,8},{8,0},{1,9},{9,1},{2,10},{10,2},{3,11},{11,3},{4,12},{12,4},... | collective-permute-start | bytes 3145736 | tf_op jit(solution)/shard_map/ppermute | solution.py:309
  4.1 2.8 %collective-permute-done.g_other = bf16[1024,512]{1,0:T(8,128)(2,1)S(1)} collective-permute-done((bf16[1024,512]{1,0:T(8,128)(2,1)}, bf16[1024,512]{1,0:T(8,128)(2,1)S(1)}, u32[]{:S(2)}, u32[]{:S(2)}) %collective-permute-start) | collective-permute-done | bytes 1048608 | tf_op jit(solution)/shard_map/ppermute | solution.py:309
  8.1 11.7 %whiten.1 = (bf16[1024,1664]{1,0:T(8,128)(2,1)}, f32[1,1]{1,0:T(1,128)}, f32[64,640]{1,0:T(8,128)S(1)}, f32[64,640]{1,0:T(8,128)S(1)}, f32[64,640]{1,0:T(8,128)S...) custom-call(s32[3]{0:T(128)S(1)} %pad_add_fusion.ids, ...), custom_call_target="tpu_custom_call" | custom-call | flops 5637144576 | bytes 8388608 | tf_op jit(solution)/shard_map/whiten/pallas_call | solution.py:130
  19.9 3.9 %collective-permute-start.14 = (f32[64,640]{1,0:T(8,128)S(1)}, f32[64,640]{1,0:T(8,128)S(1)}, u32[]{:S(2)}, u32[]{:S(2)}) collective-permute-start(f32[64,640]{1,0:T(8,128)S(1)} %get-tuple-element.41), channel_id=1, source_target_pairs={{0,224},{32,0},{64,32},{96,64},{128,96},{160,128},{192,160},{224,1... | collective-permute-start | bytes 491528 | tf_op jit(solution)/shard_map/ppermute | solution.py:305
  25.3 2.7 %collective-permute-done.2 = f32[64,640]{1,0:T(8,128)S(1)} collective-permute-done((f32[64,640]{1,0:T(8,128)S(1)}, f32[64,640]{1,0:T(8,128)S(1)}, u32[]{:S(2)}, u32[]{:S(2)}) %collective-permute-start.2) | collective-permute-done | bytes 163872 | tf_op jit(solution)/shard_map/ppermute | solution.py:305
  28.1 2.7 %collective-permute-start.15 = (f32[64,640]{1,0:T(8,128)S(1)}, f32[64,640]{1,0:T(8,128)S(1)}, u32[]{:S(2)}, u32[]{:S(2)}) collective-permute-start(f32[64,640]{1,0:T(8,128)S(1)} %add.84), channel_id=1, source_target_pairs={{0,224},{32,0},{64,32},{96,64},{128,96},{160,128},{192,160},{224,1... | collective-permute-start | bytes 491528 | tf_op jit(solution)/shard_map/ppermute | solution.py:305
  30.9 3.1 %collective-permute-start.7 = (f32[64,640]{1,0:T(8,128)S(1)}, f32[64,640]{1,0:T(8,128)S(1)}, u32[]{:S(2)}, u32[]{:S(2)}) collective-permute-start(f32[64,640]{1,0:T(8,128)S(1)} %add.73), channel_id=1, source_target_pairs={{0,224},{32,0},{64,32},{96,64},{128,96},{160,128},{192,160},{224,1... | collective-permute-start | bytes 491528 | tf_op jit(solution)/shard_map/ppermute | solution.py:305
  35.5 2.9 %collective-permute-start.16 = (f32[64,640]{1,0:T(8,128)S(1)}, f32[64,640]{1,0:T(8,128)S(1)}, u32[]{:S(2)}, u32[]{:S(2)}) collective-permute-start(f32[64,640]{1,0:T(8,128)S(1)} %add.85), channel_id=1, source_target_pairs={{0,224},{32,0},{64,32},{96,64},{128,96},{160,128},{192,160},{224,1... | collective-permute-start | bytes 491528 | tf_op jit(solution)/shard_map/ppermute | solution.py:305
  38.4 2.0 %collective-permute-start.9 = (f32[32,1024]{1,0:T(8,128)S(1)}, f32[32,1024]{1,0:T(8,128)S(1)}, u32[]{:S(2)}, u32[]{:S(2)}) collective-permute-start(f32[32,1024]{1,0:T(8,128)S(1)} %get-tuple-element.58), channel_id=1, source_target_pairs={{0,8},{8,0},{1,9},{9,1},{2,10},{10,2},{3,11},{11,3},{4,12},{12,4},... | collective-permute-start | bytes 393224 | tf_op jit(solution)/shard_map/ppermute | solution.py:309
  43.2 2.7 %collective-permute-start.17 = (f32[64,640]{1,0:T(8,128)S(1)}, f32[64,640]{1,0:T(8,128)S(1)}, u32[]{:S(2)}, u32[]{:S(2)}) collective-permute-start(f32[64,640]{1,0:T(8,128)S(1)} %add.86), channel_id=1, source_target_pairs={{0,224},{32,0},{64,32},{96,64},{128,96},{160,128},{192,160},{224,1... | collective-permute-start | bytes 491528 | tf_op jit(solution)/shard_map/ppermute | solution.py:305
  46.7 2.8 %collective-permute-done.5 = f32[64,640]{1,0:T(8,128)S(1)} collective-permute-done((f32[64,640]{1,0:T(8,128)S(1)}, f32[64,640]{1,0:T(8,128)S(1)}, u32[]{:S(2)}, u32[]{:S(2)}) %collective-permute-start.5) | collective-permute-done | bytes 163872 | tf_op jit(solution)/shard_map/ppermute | solution.py:305
  51.1 2.7 %collective-permute-done.18 = f32[64,640]{1,0:T(8,128)S(1)} collective-permute-done((f32[64,640]{1,0:T(8,128)S(1)}, f32[64,640]{1,0:T(8,128)S(1)}, u32[]{:S(2)}, u32[]{:S(2)}) %collective-permute-start.18) | collective-permute-done | bytes 163872 | tf_op jit(solution)/shard_map/ppermute | solution.py:309
  53.9 1.9 %collective-permute-start.20 = (f32[64,640]{1,0:T(8,128)S(1)}, f32[64,640]{1,0:T(8,128)S(1)}, u32[]{:S(2)}, u32[]{:S(2)}) collective-permute-start(f32[64,640]{1,0:T(8,128)S(1)} %add.89.refs_1_), channel_id=1, source_target_pairs={{0,224},{32,0},{64,32},{96,64},{128,96},{160,128},{192,160},{224,1... | collective-permute-start | bytes 491528 | tf_op jit(solution)/shard_map/ppermute | solution.py:305
  57.9 2.0 %collective-permute-start.19 = (f32[64,640]{1,0:T(8,128)S(1)}, f32[64,640]{1,0:T(8,128)S(1)}, u32[]{:S(2)}, u32[]{:S(2)}) collective-permute-start(f32[64,640]{1,0:T(8,128)S(1)} %add.80.refs_0_), channel_id=1, source_target_pairs={{0,224},{32,0},{64,32},{96,64},{128,96},{160,128},{192,160},{224,1... | collective-permute-start | bytes 491528 | tf_op jit(solution)/shard_map/ppermute | solution.py:305
  59.9 3.4 %collective-permute-start.22 = (f32[64,640]{1,0:T(8,128)S(1)}, f32[64,640]{1,0:T(8,128)S(1)}, u32[]{:S(2)}, u32[]{:S(2)}) collective-permute-start(f32[64,640]{1,0:T(8,128)S(1)} %collective-permute-done.20.refs_3_), channel_id=1, source_target_pairs={{0,224},{32,0},{64,32},{96,64},{128,96},{160,128},{192,160},{224,1... | collective-permute-start | bytes 491528 | tf_op jit(solution)/shard_map/ppermute | solution.py:305
  64.8 4.7 %collective-permute-start.21 = (f32[64,640]{1,0:T(8,128)S(1)}, f32[64,640]{1,0:T(8,128)S(1)}, u32[]{:S(2)}, u32[]{:S(2)}) collective-permute-start(f32[64,640]{1,0:T(8,128)S(1)} %collective-permute-done.19.refs_2_), channel_id=1, source_target_pairs={{0,224},{32,0},{64,32},{96,64},{128,96},{160,128},{192,160},{224,1... | collective-permute-start | bytes 491528 | tf_op jit(solution)/shard_map/ppermute | solution.py:305
  72.7 3.7 %collective-permute-start.23 = (f32[64,640]{1,0:T(8,128)S(1)}, f32[64,640]{1,0:T(8,128)S(1)}, u32[]{:S(2)}, u32[]{:S(2)}) collective-permute-start(f32[64,640]{1,0:T(8,128)S(1)} %collective-permute-done.21.refs_4_), channel_id=1, source_target_pairs={{0,224},{32,0},{64,32},{96,64},{128,96},{160,128},{192,160},{224,1... | collective-permute-start | bytes 491528 | tf_op jit(solution)/shard_map/ppermute | solution.py:305
  77.8 2.0 %collective-permute-done.32.refs_11_ = f32[64,640]{1,0:T(8,128)S(1)} collective-permute-done((f32[64,640]{1,0:T(8,128)S(1)}, f32[64,640]{1,0:T(8,128)S(1)}, u32[]{:S(2)}, u32[]{:S(2)}) %collective-permute-start.32) | collective-permute-done | bytes 163872 | tf_op jit(solution)/shard_map/ppermute | solution.py:305
  82.0 2.0 %collective-permute-done.28.refs_8_ = f32[64,640]{1,0:T(8,128)S(1)} collective-permute-done((f32[64,640]{1,0:T(8,128)S(1)}, f32[64,640]{1,0:T(8,128)S(1)}, u32[]{:S(2)}, u32[]{:S(2)}) %collective-permute-start.28) | collective-permute-done | bytes 163872 | tf_op jit(solution)/shard_map/ppermute | solution.py:305
  84.1 24.7 %root.1 = (f32[512,1024]{1,0:T(8,128)S(1)}, f32[512,1024]{1,0:T(8,128)}, f32[128,1024]{1,0:T(8,128)S(1)}, f32[256,1,128]{2,1,0:T(1,128)}) custom-call(s32[3]{0:T(128)S(1)} %pad_add_fusion.ids, f32[1,1]{1,0:T(1,128)} %get-tuple-element.25.gsq, f32[64,640]{1,0:T(8,128)S(1)} %add.80.refs_0_, f32[64,640]{1,0:T(8,128)S(1)} %add.89.refs_1_, ...), custom_call_target="tpu_custom_call" | custom-call | flops 15032385536 | bytes 8388608 | tf_op jit(solution)/shard_map/root/pallas_call | solution.py:252
  108.8 6.7 %collective-permute-start.33 = (f32[512,1024]{1,0:T(8,128)}, f32[512,1024]{1,0:T(8,128)}, u32[]{:S(2)}, u32[]{:S(2)}) collective-permute-start(f32[512,1024]{1,0:T(8,128)} %get-tuple-element.45), channel_id=1, source_target_pairs={{0,8},{8,0},{1,9},{9,1},{2,10},{10,2},{3,11},{11,3},{4,12},{12,4},... | collective-permute-start | bytes 6291464 | tf_op jit(solution)/shard_map/ppermute | solution.py:309
  115.7 14.5 %all-to-all-start = ((f32[256,1,128]{2,1,0:T(1,128)}), f32[256,1,128]{2,1,0:T(1,128)S(1)}, u32[]{:S(2)}, u32[]{:S(2)}) async-start(f32[256,1,128]{2,1,0:T(1,128)} %get-tuple-element.43), calls=%async_computation | async-start | bytes 262144 | tf_op jit(solution)/shard_map/all_to_all | solution.py:375
  131.1 12.2 %all-to-all-done.squares = f32[256,1,128]{2,1,0:T(1,128)S(1)} async-done(((f32[256,1,128]{2,1,0:T(1,128)}), f32[256,1,128]{2,1,0:T(1,128)S(1)}, u32[]{:S(2)}, u32[]{:S(2)}) %all-to-all-start) | async-done | bytes 131104 | tf_op jit(solution)/shard_map/all_to_all | solution.py:375
  143.2 4.9 %finish.1 = bf16[512,2048]{1,0:T(8,128)(2,1)} custom-call(s32[3]{0:T(128)S(1)} %pad_add_fusion.ids, f32[256,1,128]{2,1,0:T(1,128)S(1)} %all-to-all-done.squares, f32[512,1024]{1,0:T(8,128)S(1)} %get-tuple-element.44.own, f32[512,1024]{1,0:T(8,128)} %collective-permute-done.33.other), custom_call_target="tpu_custom_call" | custom-call | tf_op jit(solution)/shard_map/finish/pallas_call | solution.py:284
  (75 shorter events, 21.2 us)
Async XLA Ops:
  19.8 8.2 %collective-permute-start.2 = (f32[64,640]{1,0:T(8,128)S(1)}, f32[64,640]{1,0:T(8,128)S(1)}, u32[]{:S(2)}, u32[]{:S(2)}) collective-permute-start(f32[64,640]{1,0:T(8,128)S(1)} %get-tuple-element.30), channel_id=1, source_target_pairs={{0,32},{32,64},{64,96},{96,128},{128,160},{160,192},{192,224},{224... | collective-permute-start | bytes 491528 | tf_op jit(solution)/shard_map/ppermute | solution.py:305
  19.9 8.2 %collective-permute-start.14 = (f32[64,640]{1,0:T(8,128)S(1)}, f32[64,640]{1,0:T(8,128)S(1)}, u32[]{:S(2)}, u32[]{:S(2)}) collective-permute-start(f32[64,640]{1,0:T(8,128)S(1)} %get-tuple-element.41), channel_id=1, source_target_pairs={{0,224},{32,0},{64,32},{96,64},{128,96},{160,128},{192,160},{224,1... | collective-permute-start | bytes 491528 | tf_op jit(solution)/shard_map/ppermute | solution.py:305
  23.8 7.1 %collective-permute-start.6 = (f32[64,640]{1,0:T(8,128)S(1)}, f32[64,640]{1,0:T(8,128)S(1)}, u32[]{:S(2)}, u32[]{:S(2)}) collective-permute-start(f32[64,640]{1,0:T(8,128)S(1)} %get-tuple-element.33), channel_id=1, source_target_pairs={{0,224},{32,0},{64,32},{96,64},{128,96},{160,128},{192,160},{224,1... | collective-permute-start | bytes 491528 | tf_op jit(solution)/shard_map/ppermute | solution.py:305
  25.2 8.9 %collective-permute-start.11 = (f32[64,640]{1,0:T(8,128)S(1)}, f32[64,640]{1,0:T(8,128)S(1)}, u32[]{:S(2)}, u32[]{:S(2)}) collective-permute-start(f32[64,640]{1,0:T(8,128)S(1)} %get-tuple-element.37), channel_id=1, source_target_pairs={{0,32},{32,64},{64,96},{96,128},{128,160},{160,192},{192,224},{224... | collective-permute-start | bytes 491528 | tf_op jit(solution)/shard_map/ppermute | solution.py:305
  28.0 7.3 %collective-permute-start.3 = (f32[64,640]{1,0:T(8,128)S(1)}, f32[64,640]{1,0:T(8,128)S(1)}, u32[]{:S(2)}, u32[]{:S(2)}) collective-permute-start(f32[64,640]{1,0:T(8,128)S(1)} %add.69), channel_id=1, source_target_pairs={{0,32},{32,64},{64,96},{96,128},{128,160},{160,192},{192,224},{224... | collective-permute-start | bytes 491528 | tf_op jit(solution)/shard_map/ppermute | solution.py:305
  28.1 7.3 %collective-permute-start.15 = (f32[64,640]{1,0:T(8,128)S(1)}, f32[64,640]{1,0:T(8,128)S(1)}, u32[]{:S(2)}, u32[]{:S(2)}) collective-permute-start(f32[64,640]{1,0:T(8,128)S(1)} %add.84), channel_id=1, source_target_pairs={{0,224},{32,0},{64,32},{96,64},{128,96},{160,128},{192,160},{224,1... | collective-permute-start | bytes 491528 | tf_op jit(solution)/shard_map/ppermute | solution.py:305
  30.9 9.5 %collective-permute-start.7 = (f32[64,640]{1,0:T(8,128)S(1)}, f32[64,640]{1,0:T(8,128)S(1)}, u32[]{:S(2)}, u32[]{:S(2)}) collective-permute-start(f32[64,640]{1,0:T(8,128)S(1)} %add.73), channel_id=1, source_target_pairs={{0,224},{32,0},{64,32},{96,64},{128,96},{160,128},{192,160},{224,1... | collective-permute-start | bytes 491528 | tf_op jit(solution)/shard_map/ppermute | solution.py:305
  34.1 7.2 %collective-permute-start.12 = (f32[64,640]{1,0:T(8,128)S(1)}, f32[64,640]{1,0:T(8,128)S(1)}, u32[]{:S(2)}, u32[]{:S(2)}) collective-permute-start(f32[64,640]{1,0:T(8,128)S(1)} %add.81), channel_id=1, source_target_pairs={{0,32},{32,64},{64,96},{96,128},{128,160},{160,192},{192,224},{224... | collective-permute-start | bytes 491528 | tf_op jit(solution)/shard_map/ppermute | solution.py:305
  35.4 7.7 %collective-permute-start.4 = (f32[64,640]{1,0:T(8,128)S(1)}, f32[64,640]{1,0:T(8,128)S(1)}, u32[]{:S(2)}, u32[]{:S(2)}) collective-permute-start(f32[64,640]{1,0:T(8,128)S(1)} %add.70), channel_id=1, source_target_pairs={{0,32},{32,64},{64,96},{96,128},{128,160},{160,192},{192,224},{224... | collective-permute-start | bytes 491528 | tf_op jit(solution)/shard_map/ppermute | solution.py:305
  35.5 7.7 %collective-permute-start.16 = (f32[64,640]{1,0:T(8,128)S(1)}, f32[64,640]{1,0:T(8,128)S(1)}, u32[]{:S(2)}, u32[]{:S(2)}) collective-permute-start(f32[64,640]{1,0:T(8,128)S(1)} %add.85), channel_id=1, source_target_pairs={{0,224},{32,0},{64,32},{96,64},{128,96},{160,128},{192,160},{224,1... | collective-permute-start | bytes 491528 | tf_op jit(solution)/shard_map/ppermute | solution.py:305
  38.4 7.5 %collective-permute-start.9 = (f32[32,1024]{1,0:T(8,128)S(1)}, f32[32,1024]{1,0:T(8,128)S(1)}, u32[]{:S(2)}, u32[]{:S(2)}) collective-permute-start(f32[32,1024]{1,0:T(8,128)S(1)} %get-tuple-element.58), channel_id=1, source_target_pairs={{0,8},{8,0},{1,9},{9,1},{2,10},{10,2},{3,11},{11,3},{4,12},{12,4},... | collective-permute-start | bytes 393224 | tf_op jit(solution)/shard_map/ppermute | solution.py:309
  55.8 7.5 %collective-permute-start.25 = (f32[64,640]{1,0:T(8,128)S(1)}, f32[64,640]{1,0:T(8,128)S(1)}, u32[]{:S(2)}, u32[]{:S(2)}) collective-permute-start(f32[64,640]{1,0:T(8,128)S(1)} %add.80.refs_0_), channel_id=1, source_target_pairs={{0,32},{32,64},{64,96},{96,128},{128,160},{160,192},{192,224},{224... | collective-permute-start | bytes 491528 | tf_op jit(solution)/shard_map/ppermute | solution.py:305
  56.1 8.0 %collective-permute-start.30 = (f32[64,640]{1,0:T(8,128)S(1)}, f32[64,640]{1,0:T(8,128)S(1)}, u32[]{:S(2)}, u32[]{:S(2)}) collective-permute-start(f32[64,640]{1,0:T(8,128)S(1)} %add.89.refs_1_), channel_id=1, source_target_pairs={{0,32},{32,64},{64,96},{96,128},{128,160},{160,192},{192,224},{224... | collective-permute-start | bytes 491528 | tf_op jit(solution)/shard_map/ppermute | solution.py:305
  59.9 9.6 %collective-permute-start.22 = (f32[64,640]{1,0:T(8,128)S(1)}, f32[64,640]{1,0:T(8,128)S(1)}, u32[]{:S(2)}, u32[]{:S(2)}) collective-permute-start(f32[64,640]{1,0:T(8,128)S(1)} %collective-permute-done.20.refs_3_), channel_id=1, source_target_pairs={{0,224},{32,0},{64,32},{96,64},{128,96},{160,128},{192,160},{224,1... | collective-permute-start | bytes 491528 | tf_op jit(solution)/shard_map/ppermute | solution.py:305
  63.3 7.6 %collective-permute-start.26 = (f32[64,640]{1,0:T(8,128)S(1)}, f32[64,640]{1,0:T(8,128)S(1)}, u32[]{:S(2)}, u32[]{:S(2)}) collective-permute-start(f32[64,640]{1,0:T(8,128)S(1)} %collective-permute-done.25.refs_14_), channel_id=1, source_target_pairs={{0,32},{32,64},{64,96},{96,128},{128,160},{160,192},{192,224},{224... | collective-permute-start | bytes 491528 | tf_op jit(solution)/shard_map/ppermute | solution.py:305
  64.1 8.5 %collective-permute-start.31 = (f32[64,640]{1,0:T(8,128)S(1)}, f32[64,640]{1,0:T(8,128)S(1)}, u32[]{:S(2)}, u32[]{:S(2)}) collective-permute-start(f32[64,640]{1,0:T(8,128)S(1)} %collective-permute-done.30.refs_15_), channel_id=1, source_target_pairs={{0,32},{32,64},{64,96},{96,128},{128,160},{160,192},{192,224},{224... | collective-permute-start | bytes 491528 | tf_op jit(solution)/shard_map/ppermute | solution.py:305
  64.8 7.9 %collective-permute-start.21 = (f32[64,640]{1,0:T(8,128)S(1)}, f32[64,640]{1,0:T(8,128)S(1)}, u32[]{:S(2)}, u32[]{:S(2)}) collective-permute-start(f32[64,640]{1,0:T(8,128)S(1)} %collective-permute-done.19.refs_2_), channel_id=1, source_target_pairs={{0,224},{32,0},{64,32},{96,64},{128,96},{160,128},{192,160},{224,1... | collective-permute-start | bytes 491528 | tf_op jit(solution)/shard_map/ppermute | solution.py:305
  69.4 6.9 %collective-permute-start.24 = (f32[64,640]{1,0:T(8,128)S(1)}, f32[64,640]{1,0:T(8,128)S(1)}, u32[]{:S(2)}, u32[]{:S(2)}) collective-permute-start(f32[64,640]{1,0:T(8,128)S(1)} %collective-permute-done.22.refs_5_), channel_id=1, source_target_pairs={{0,224},{32,0},{64,32},{96,64},{128,96},{160,128},{192,160},{224,1... | collective-permute-start | bytes 491528 | tf_op jit(solution)/shard_map/ppermute | solution.py:305
  70.9 6.9 %collective-permute-start.27 = (f32[64,640]{1,0:T(8,128)S(1)}, f32[64,640]{1,0:T(8,128)S(1)}, u32[]{:S(2)}, u32[]{:S(2)}) collective-permute-start(f32[64,640]{1,0:T(8,128)S(1)} %collective-permute-done.26.refs_12_), channel_id=1, source_target_pairs={{0,32},{32,64},{64,96},{96,128},{128,160},{160,192},{192,224},{224... | collective-permute-start | bytes 491528 | tf_op jit(solution)/shard_map/ppermute | solution.py:305
  72.7 7.1 %collective-permute-start.32 = (f32[64,640]{1,0:T(8,128)S(1)}, f32[64,640]{1,0:T(8,128)S(1)}, u32[]{:S(2)}, u32[]{:S(2)}) collective-permute-start(f32[64,640]{1,0:T(8,128)S(1)} %collective-permute-done.31.refs_13_), channel_id=1, source_target_pairs={{0,32},{32,64},{64,96},{96,128},{128,160},{160,192},{192,224},{224... | collective-permute-start | bytes 491528 | tf_op jit(solution)/shard_map/ppermute | solution.py:305
  72.7 7.6 %collective-permute-start.23 = (f32[64,640]{1,0:T(8,128)S(1)}, f32[64,640]{1,0:T(8,128)S(1)}, u32[]{:S(2)}, u32[]{:S(2)}) collective-permute-start(f32[64,640]{1,0:T(8,128)S(1)} %collective-permute-done.21.refs_4_), channel_id=1, source_target_pairs={{0,224},{32,0},{64,32},{96,64},{128,96},{160,128},{192,160},{224,1... | collective-permute-start | bytes 491528 | tf_op jit(solution)/shard_map/ppermute | solution.py:305
  108.8 34.5 %collective-permute-start.33 = (f32[512,1024]{1,0:T(8,128)}, f32[512,1024]{1,0:T(8,128)}, u32[]{:S(2)}, u32[]{:S(2)}) collective-permute-start(f32[512,1024]{1,0:T(8,128)} %get-tuple-element.45), channel_id=1, source_target_pairs={{0,8},{8,0},{1,9},{9,1},{2,10},{10,2},{3,11},{11,3},{4,12},{12,4},... | collective-permute-start | bytes 6291464 | tf_op jit(solution)/shard_map/ppermute | solution.py:309
  115.5 14.7 %collective-permute-start.34 = (f32[64,1024]{1,0:T(8,128)S(1)}, f32[64,1024]{1,0:T(8,128)S(1)}, u32[]{:S(2)}, u32[]{:S(2)}) collective-permute-start(f32[64,1024]{1,0:T(8,128)S(1)} %get-tuple-element.54), channel_id=1, source_target_pairs={{0,8},{8,0},{1,9},{9,1},{2,10},{10,2},{3,11},{11,3},{4,12},{12,4},... | collective-permute-start | bytes 786440 | tf_op jit(solution)/shard_map/ppermute | solution.py:309
  115.7 27.6 %all-to-all-start = ((f32[256,1,128]{2,1,0:T(1,128)}), f32[256,1,128]{2,1,0:T(1,128)S(1)}, u32[]{:S(2)}, u32[]{:S(2)}) async-start(f32[256,1,128]{2,1,0:T(1,128)} %get-tuple-element.43), calls=%async_computation | async-start | bytes 262144 | tf_op jit(solution)/shard_map/all_to_all | solution.py:375
  (14 other events, 87.9 us)
